TPU v7x, 256 devices: a whole 4x4x8 slice. The times are simulated.
256 devices in a mesh: types: 128 (over x, z, y), tm: 2 (over core).
Axes of the slice: x: 4, y: 4, z: 8, core: 2. Of those that a mesh axis runs over, the one named last changes fastest.
Arguments:
- brackets: int32 [768, 8, 7, 512], P('types', 'tm'), may hold values from 0 to 510, as said below
- active_blocks: int32 [768], P('types'), may hold values from 1 to 4, as said below
- initial_mass: float32 [768, 7, 512], P('types'), may hold values from 0 to 0.00055803574
- patience: float32 [768], P('types'), may hold values from 0.9 to 0.985
- productivity: float32 [768], P('types'), may hold values from 0.5 to 2
- income_levels: float32 [7], replicated, may hold values from 0.3 to 3
- income_transition: float32 [7, 7], replicated, may hold values from 0 to 1, as said below
- wage_path: float32 [8], replicated, may hold values from 0.8 to 1.2
- bond_supply: float32 [8], replicated, may hold values from 0.5 to 2
- price_guess: float32 [8], replicated, may hold values from -3 to 3
- jac_inverse: float32 [8, 8], replicated, may hold values from -2 to 2
- assignment: int32 [768], replicated, may hold values from 0 to 767, each once
Outputs:
- price_path: float32 [8], replicated
- market_gap: float32 [8], replicated
- type_paths: float32 [768, 2, 8], P('types')
Inputs may be any that keep to these rules, and one draw needn't show every extreme that they name: `brackets`: the bracket of asset point i lies between max(i - 9, 0) and max(i - 1, 0). `active_blocks`: counts of 128-point blocks from the bottom of the grid. `income_transition`: rows of positive entries summing to one. `assignment`: each type appears once.
All inputs are finite; a program needn't handle non-finite values.
Results may differ from a plain program's by a relative error of at most 0.0003.
Values sent between devices are 32-bit elements; how exact they have to be, the bound alone decides.
No kernel may reach another device: no remote copies, remote signals or barrier semaphores. Data moves between devices by JAX's collectives and lax.ppermute only.
A program may use at most 64 MiB of HBM per device.

v0:
```python
import functools
import math

import jax
import jax.numpy as jnp
from jax import lax
from jax.sharding import Mesh
from jax.sharding import PartitionSpec as P

ASSETS = 512
BLOCK = 128
NEWTON = 2
TYPES = ("types_0", "types_1", "types_2")
TYPES_TM = ("types_0", "types_1", "types_2", "tm")


grid_top = 40.0
rate_floor = 0.005
rate_span = 0.03
highest = lax.Precision.HIGHEST


def sent_together(arrays, axis, dim, along):
    widths = [math.prod(a.shape[along:]) for a in arrays]
    both = jnp.concatenate(
        [a.reshape(*a.shape[:along], w) for a, w in zip(arrays, widths)], axis=along
    )
    whole = lax.all_gather(both, axis, axis=dim, tiled=True)
    pieces = jnp.split(whole, [sum(widths[:k]) for k in range(1, len(widths))], axis=along)
    return tuple(
        (b.reshape(*whole.shape[:along], *a.shape[along:]) for a, b in zip(arrays, pieces))
    )


def over_axes(array, axes):
    return functools.reduce(lax.psum, axes, array)


def asset_grid(points):
    return grid_top * (points / (ASSETS - 1)) ** 2


def interest(price_path):
    return rate_floor + rate_span * jax.nn.sigmoid(price_path)


def policy(lower_edge, upper_edge, bracket_now, rate_now, income_now, grid_rows):
    grid_low = asset_grid(bracket_now.astype(jnp.float32))
    grid_high = asset_grid((bracket_now + 1).astype(jnp.float32))
    spacing = jnp.maximum(upper_edge - lower_edge, (grid_high - grid_low) / (1.0 + rate_now))
    weight_up = jnp.clip((grid_rows[None, :] - lower_edge) / spacing, 0.0, 1.0)
    savings = grid_low + weight_up * (grid_high - grid_low)
    spending = (1.0 + rate_now) * grid_rows[None, :] + income_now[:, None] - savings
    return (weight_up, savings, spending)


def band_table(bracket_rows, window):
    targets = window + jnp.arange(2 * BLOCK, dtype=jnp.int32)
    return (bracket_rows[:, :, None] == targets[None, None, :]).astype(jnp.float32)


def backward_type(bracket, blocks, patience, incomes, interest_path, values_end, transition):
    grid_values = asset_grid(jnp.arange(ASSETS, dtype=jnp.float32))
    income_count = values_end.shape[0]

    def backward_period(values, inputs):
        bracket_now, rate_now, income_now = inputs
        expected = patience * jnp.dot(transition, values, precision=highest)
        endogenous = (1.0 / expected + grid_values[None, :] - income_now[:, None]) / (
            1.0 + rate_now
        )
        following = jnp.concatenate([endogenous[:, 1:], endogenous[:, -1:]], axis=1)
        stacked = jnp.stack([endogenous, following])

        def backward_block_rows(block_index, carried):
            row_start = block_index * BLOCK
            window = jnp.maximum(row_start - BLOCK, 0)
            bracket_rows = lax.dynamic_slice_in_dim(bracket_now, row_start, BLOCK, 1)
            onehot = band_table(bracket_rows, window)
            stacked_window = lax.dynamic_slice_in_dim(stacked, window, 2 * BLOCK, 2)
            picked = jnp.einsum("eia,cea->cei", onehot, stacked_window, precision=highest)
            grid_rows = lax.dynamic_slice_in_dim(grid_values, row_start, BLOCK, 0)
            weight_up, savings, spending = policy(
                picked[0], picked[1], bracket_rows, rate_now, income_now, grid_rows
            )
            fresh = (weight_up, savings, spending, (1.0 + rate_now) / spending)
            return tuple(
                (
                    lax.dynamic_update_slice_in_dim(target_array, piece_array, row_start, 1)
                    for target_array, piece_array in zip(carried, fresh)
                )
            )

        zeros_rows = jnp.zeros((income_count, ASSETS), jnp.float32)
        ones_rows = jnp.ones((income_count, ASSETS), jnp.float32)
        weight_up, savings, spending, values_new = lax.fori_loop(
            0, blocks, backward_block_rows, (zeros_rows, zeros_rows, ones_rows, ones_rows)
        )
        return (values_new, (weight_up, savings, spending))

    return lax.scan(backward_period, values_end, (bracket, interest_path, incomes), reverse=True)


def forward_type(bracket, blocks, weight_up, savings, spending, mass_start, transition):

    def forward_period(masses, inputs):
        bracket_now, weight_now, savings_now, spending_now = inputs
        totals = jnp.stack([jnp.sum(masses * savings_now), jnp.sum(masses * spending_now)])
        weights = jnp.stack([(1.0 - weight_now) * masses, weight_now * masses])

        def forward_block_rows(block_index, shifted_mass):
            row_start = block_index * BLOCK
            window = jnp.maximum(row_start - BLOCK, 0)
            bracket_rows = lax.dynamic_slice_in_dim(bracket_now, row_start, BLOCK, 1)
            onehot = band_table(bracket_rows, window)
            weight_rows = lax.dynamic_slice_in_dim(weights, row_start, BLOCK, 2)
            contrib = jnp.einsum("eia,cei->cea", onehot, weight_rows, precision=highest)
            current = lax.dynamic_slice_in_dim(shifted_mass, window, 2 * BLOCK, 2)
            return lax.dynamic_update_slice_in_dim(shifted_mass, current + contrib, window, 2)

        shifted_mass = lax.fori_loop(0, blocks, forward_block_rows, jnp.zeros_like(weights))
        arrived = shifted_mass[0] + jnp.concatenate(
            [jnp.zeros_like(shifted_mass[1][:, :1]), shifted_mass[1][:, :-1]], axis=1
        )
        return (jnp.dot(transition.T, arrived, precision=highest), totals)

    masses_end, type_series = lax.scan(
        forward_period, mass_start, (bracket, weight_up, savings, spending)
    )
    return (masses_end, type_series.T)


def body(
    brackets,
    active_blocks,
    initial_mass,
    patience,
    productivity,
    income_levels,
    income_transition,
    wage_path,
    bond_supply,
    price_guess,
    jac_inverse,
    assignment,
):
    local_types = patience.shape[0]
    all_types = local_types * lax.axis_size(TYPES)
    core_count = lax.axis_size("tm")
    core_index = lax.axis_index("tm")
    columns = jnp.arange(ASSETS, dtype=jnp.int32)
    grid_values = asset_grid(columns.astype(jnp.float32))
    type_numbers = (
        lax.axis_index(TYPES) * local_types + jnp.arange(local_types, dtype=jnp.int32)
    ).astype(jnp.float32)
    half_types = local_types // core_count
    brackets_mine = lax.all_to_all(brackets, "tm", split_axis=0, concat_axis=1, tiled=True)

    def take_mine(target_array):
        return lax.dynamic_slice_in_dim(target_array, core_index * half_types, half_types, 0)

    blocks_mine = take_mine(active_blocks)
    patience_mine = take_mine(patience)
    productivity_mine = take_mine(productivity)
    mass_mine = take_mine(initial_mass)
    numbers_mine = take_mine(type_numbers)
    live_rows = (columns[None, None, :] < blocks_mine[:, None, None] * BLOCK).astype(jnp.float32)
    mass_start = mass_mine * live_rows
    price_path = price_guess
    market_gap = jnp.zeros_like(price_guess)
    everything = None
    for newton_round in range(NEWTON):
        interest_path = interest(price_path)
        last_rate = interest_path[-1]
        ends_income = wage_path[-1] * productivity_mine[:, None] * income_levels[None, :]
        values_end = (1.0 + last_rate) / (
            last_rate * grid_values[None, None, :] + ends_income[:, :, None]
        )
        interest_here = interest_path
        incomes = (
            wage_path[None, :, None]
            * productivity_mine[:, None, None]
            * income_levels[None, None, :]
        )

        def sweep_solve_member(members):
            return backward_type(
                members[0],
                members[1],
                members[2],
                members[3],
                interest_here,
                members[4],
                income_transition,
            )

        values_start, solve_policies = lax.map(
            sweep_solve_member, (brackets_mine, blocks_mine, patience_mine, incomes, values_end)
        )

        def solve_member(members):
            return forward_type(
                members[0],
                members[1],
                members[2],
                members[3],
                members[4],
                members[5],
                income_transition,
            )

        masses_end, solve_type_series = lax.map(
            solve_member,
            (
                brackets_mine,
                blocks_mine,
                solve_policies[0],
                solve_policies[1],
                solve_policies[2],
                mass_start,
            ),
        )
        local_sum = jnp.sum(solve_type_series[:, 0, :], axis=0)
        totals = over_axes(local_sum, TYPES_TM)
        if newton_round + 1 == NEWTON:
            everything = sent_together((solve_type_series, numbers_mine), TYPES_TM, 0, 1)
        market_gap = totals / all_types - bond_supply
        price_path = price_path - jnp.dot(jac_inverse, market_gap, precision=highest)
    slot_types = lax.dynamic_slice_in_dim(
        assignment, lax.axis_index(TYPES) * local_types, local_types, 0
    ).astype(jnp.float32)
    select = (slot_types[:, None] == everything[1][None, :]).astype(jnp.float32)
    type_paths = jnp.einsum("st,tcp->scp", select, everything[0], precision=highest)
    return (price_path, market_gap, type_paths)


def solution(mesh):
    torus = Mesh(
        mesh.devices.reshape(4, 8, 4, mesh.shape["tm"]), ("types_0", "types_1", "types_2", "tm")
    )
    in_specs = (
        P(TYPES, "tm", None, None),
        P(TYPES),
        P(TYPES, None, None),
        P(TYPES),
        P(TYPES),
        P(),
        P(),
        P(),
        P(),
        P(),
        P(),
        P(),
    )
    out_specs = (P(), P(), P(TYPES, None, None))
    return jax.shard_map(body, mesh=torus, in_specs=in_specs, out_specs=out_specs, check_vma=False)
```

profile of v0, /device:TPU:1, one launch (start us, length us, event | category | flops | bytes accessed | tf_op | source)
XLA Modules:
  0.0 1006.6 jit_solution(8013964373807709494)
XLA Ops:
  0.6 6.7 all-to-all-start
  15.4 214.3 %while.321 = (s32[]{:T(128)}, f32[3,8,7,512]{3,2,1,0:T(8,128)S(1)}, f32[3,8,7,512]{3,2,1,0:T(8,128)S(1)}, f32[3,8,7,512]{3,2,1,0:T(8,128)S(1)}, f32[3,7,512]{2,1...) while((s32[]{:T(128)}, f32[3,8,7,512]{3,2,1,0:T(8,128)S(1)}, ...), condition=%wide.region_5.6_spmd, body=%wide.region_0.5_spmd.sunk | while | flops 6097422 | bytes 1872705 | solution.py:197
  16.7 70.0 %while.328 = (s32[]{:T(128)}, f32[7,512]{1,0:T(8,128)S(1)}, f32[8,7,512]{2,1,0:T(8,128)S(1)}, f32[8,7,512]{2,1,0:T(8,128)S(1)}, f32[8,7,512]{2,1,0:T(8,128)S(1)}...) while((s32[]{:T(128)}, f32[7,512]{1,0:T(8,128)S(1)}, ...), condition=%wide.region_4.4_spmd.clone.clone, body=%wide.region_1.3_spmd.clone.clone.sunk | while | flops 6097420 | bytes 483244 | solution.py:101
  19.2 6.3 while.335
  27.9 6.3 while.335
  36.7 6.3 while.335
  54.2 6.3 while.335
  62.9 6.3 while.335
  71.7 6.3 while.335
  80.4 6.3 while.335
  88.2 70.0 %while.328 = (s32[]{:T(128)}, f32[7,512]{1,0:T(8,128)S(1)}, f32[8,7,512]{2,1,0:T(8,128)S(1)}, f32[8,7,512]{2,1,0:T(8,128)S(1)}, f32[8,7,512]{2,1,0:T(8,128)S(1)}...) while((s32[]{:T(128)}, f32[7,512]{1,0:T(8,128)S(1)}, ...), condition=%wide.region_4.4_spmd.clone.clone, body=%wide.region_1.3_spmd.clone.clone.sunk | while | flops 6097420 | bytes 483244 | solution.py:101
  90.6 6.3 while.335
  99.4 6.3 while.335
  108.1 6.3 while.335
  116.9 6.3 while.335
  125.6 6.3 while.335
  134.4 6.3 while.335
  143.1 6.3 while.335
  151.9 6.3 while.335
  159.6 70.0 %while.328 = (s32[]{:T(128)}, f32[7,512]{1,0:T(8,128)S(1)}, f32[8,7,512]{2,1,0:T(8,128)S(1)}, f32[8,7,512]{2,1,0:T(8,128)S(1)}, f32[8,7,512]{2,1,0:T(8,128)S(1)}...) while((s32[]{:T(128)}, f32[7,512]{1,0:T(8,128)S(1)}, ...), condition=%wide.region_4.4_spmd.clone.clone, body=%wide.region_1.3_spmd.clone.clone.sunk | while | flops 6097420 | bytes 483244 | solution.py:101
  162.1 6.3 while.335
  170.8 6.3 while.335
  179.6 6.3 while.335
  188.3 6.3 while.335
  197.1 6.3 while.335
  205.8 6.3 while.335
  214.6 6.3 while.335
  223.3 6.3 while.335
  229.8 210.0 %while.323 = (s32[]{:T(128)}, f32[3,2,8]{2,1,0:T(2,128)S(1)}, f32[3,7,512]{2,1,0:T(8,128)S(1)}, s32[3,8,7,512]{3,2,1,0:T(8,128)S(1)}, f32[3,8,7,512]{3,2,1,0:T(8...) while((s32[]{:T(128)}, f32[3,2,8]{2,1,0:T(2,128)S(1)}, ...), condition=%wide.region_13.14_spmd, body=%wide.region_6.13_spmd.sunk | while | flops 6075148 | bytes 1450953 | solution.py:212
  230.5 69.2 %while.329 = (s32[]{:T(128)}, f32[7,512]{1,0:T(8,128)S(1)}, f32[8,2]{1,0:T(8,128)S(1)}, s32[8,7,512]{2,1,0:T(8,128)S(1)}, f32[8,7,512]{2,1,0:T(8,128)S(1)}, /*in...) while((s32[]{:T(128)}, f32[7,512]{1,0:T(8,128)S(1)}, ...), condition=%wide.region_12.12_spmd, body=%wide.region_7.11_spmd.sunk | while | flops 6075146 | bytes 502252 | solution.py:127
  300.5 69.2 %while.329 = (s32[]{:T(128)}, f32[7,512]{1,0:T(8,128)S(1)}, f32[8,2]{1,0:T(8,128)S(1)}, s32[8,7,512]{2,1,0:T(8,128)S(1)}, f32[8,7,512]{2,1,0:T(8,128)S(1)}, /*in...) while((s32[]{:T(128)}, f32[7,512]{1,0:T(8,128)S(1)}, ...), condition=%wide.region_12.12_spmd, body=%wide.region_7.11_spmd.sunk | while | flops 6075146 | bytes 502252 | solution.py:127
  370.5 69.2 %while.329 = (s32[]{:T(128)}, f32[7,512]{1,0:T(8,128)S(1)}, f32[8,2]{1,0:T(8,128)S(1)}, s32[8,7,512]{2,1,0:T(8,128)S(1)}, f32[8,7,512]{2,1,0:T(8,128)S(1)}, /*in...) while((s32[]{:T(128)}, f32[7,512]{1,0:T(8,128)S(1)}, ...), condition=%wide.region_12.12_spmd, body=%wide.region_7.11_spmd.sunk | while | flops 6075146 | bytes 502252 | solution.py:127
  445.9 10.7 %psum.57 = f32[8]{0:T(128)S(1)} all-reduce(f32[8]{0:T(128)S(1)} %psum.56), channel_id=1, replica_groups=mesh['types_0'=4,'types_1'=8,'types_2'=4,'tm'=2] {'types_1'}, use_global_device_ids=true, to_apply=%region_16.17 | all-reduce | flops 8 | bytes 64 | tf_op jit(solution)/shard_map/psum | solution.py:36
  456.5 8.6 psum.58
  465.1 9.9 psum.59
  477.3 214.4 %while.325 = (s32[]{:T(128)}, f32[3,8,7,512]{3,2,1,0:T(8,128)S(1)}, f32[3,8,7,512]{3,2,1,0:T(8,128)S(1)}, f32[3,8,7,512]{3,2,1,0:T(8,128)S(1)}, f32[3,7,512]{2,1...) while((s32[]{:T(128)}, f32[3,8,7,512]{3,2,1,0:T(8,128)S(1)}, ...), condition=%wide.region_24.25_spmd, body=%wide.region_19.24_spmd.sunk | while | flops 6097422 | bytes 1872697 | solution.py:197
  478.7 70.0 %while.330 = (s32[]{:T(128)}, f32[7,512]{1,0:T(8,128)S(1)}, f32[8,7,512]{2,1,0:T(8,128)S(1)}, f32[8,7,512]{2,1,0:T(8,128)S(1)}, f32[8,7,512]{2,1,0:T(8,128)S(1)}...) while((s32[]{:T(128)}, f32[7,512]{1,0:T(8,128)S(1)}, ...), condition=%wide.region_23.23_spmd.clone.clone, body=%wide.region_20.22_spmd.clone.clone.sunk | while | flops 6097420 | bytes 483244 | solution.py:101
  481.1 6.3 while.333
  489.9 6.3 while.333
  498.6 6.3 while.333
  507.4 6.3 while.333
  516.1 6.3 while.333
  524.9 6.3 while.333
  533.7 6.3 while.333
  550.2 70.0 %while.330 = (s32[]{:T(128)}, f32[7,512]{1,0:T(8,128)S(1)}, f32[8,7,512]{2,1,0:T(8,128)S(1)}, f32[8,7,512]{2,1,0:T(8,128)S(1)}, f32[8,7,512]{2,1,0:T(8,128)S(1)}...) while((s32[]{:T(128)}, f32[7,512]{1,0:T(8,128)S(1)}, ...), condition=%wide.region_23.23_spmd.clone.clone, body=%wide.region_20.22_spmd.clone.clone.sunk | while | flops 6097420 | bytes 483244 | solution.py:101
  552.6 6.3 while.333
  561.4 6.3 while.333
  570.1 6.3 while.333
  578.9 6.3 while.333
  587.6 6.3 while.333
  596.4 6.3 while.333
  605.1 6.3 while.333
  613.9 6.3 while.333
  621.6 70.0 %while.330 = (s32[]{:T(128)}, f32[7,512]{1,0:T(8,128)S(1)}, f32[8,7,512]{2,1,0:T(8,128)S(1)}, f32[8,7,512]{2,1,0:T(8,128)S(1)}, f32[8,7,512]{2,1,0:T(8,128)S(1)}...) while((s32[]{:T(128)}, f32[7,512]{1,0:T(8,128)S(1)}, ...), condition=%wide.region_23.23_spmd.clone.clone, body=%wide.region_20.22_spmd.clone.clone.sunk | while | flops 6097420 | bytes 483244 | solution.py:101
  632.8 6.3 while.333
  691.7 210.0 %while.327 = (s32[]{:T(128)}, f32[3,2,8]{2,1,0:T(2,128)S(1)}, f32[3,7,512]{2,1,0:T(8,128)S(1)}, s32[3,8,7,512]{3,2,1,0:T(8,128)S(1)}, f32[3,8,7,512]{3,2,1,0:T(8...) while((s32[]{:T(128)}, f32[3,2,8]{2,1,0:T(2,128)S(1)}, ...), condition=%wide.region_32.33_spmd, body=%wide.region_25.32_spmd.sunk | while | flops 6075148 | bytes 1450953 | solution.py:212
  692.4 69.2 %while.331 = (s32[]{:T(128)}, f32[7,512]{1,0:T(8,128)S(1)}, f32[8,2]{1,0:T(8,128)S(1)}, s32[8,7,512]{2,1,0:T(8,128)S(1)}, f32[8,7,512]{2,1,0:T(8,128)S(1)}, /*in...) while((s32[]{:T(128)}, f32[7,512]{1,0:T(8,128)S(1)}, ...), condition=%wide.region_31.31_spmd, body=%wide.region_26.30_spmd.sunk | while | flops 6075146 | bytes 502252 | solution.py:127
  762.4 69.2 %while.331 = (s32[]{:T(128)}, f32[7,512]{1,0:T(8,128)S(1)}, f32[8,2]{1,0:T(8,128)S(1)}, s32[8,7,512]{2,1,0:T(8,128)S(1)}, f32[8,7,512]{2,1,0:T(8,128)S(1)}, /*in...) while((s32[]{:T(128)}, f32[7,512]{1,0:T(8,128)S(1)}, ...), condition=%wide.region_31.31_spmd, body=%wide.region_26.30_spmd.sunk | while | flops 6075146 | bytes 502252 | solution.py:127
  832.4 69.2 %while.331 = (s32[]{:T(128)}, f32[7,512]{1,0:T(8,128)S(1)}, f32[8,2]{1,0:T(8,128)S(1)}, s32[8,7,512]{2,1,0:T(8,128)S(1)}, f32[8,7,512]{2,1,0:T(8,128)S(1)}, /*in...) while((s32[]{:T(128)}, f32[7,512]{1,0:T(8,128)S(1)}, ...), condition=%wide.region_31.31_spmd, body=%wide.region_26.30_spmd.sunk | while | flops 6075146 | bytes 502252 | solution.py:127
  902.1 62.6 %all-gather = f32[256,3,17]{2,1,0:T(4,128)S(1)} all-gather(f32[1,3,17]{2,1,0:T(4,128)S(1)} %maximum_bitcast_fusion.4), channel_id=1, replica_groups=mesh['types_0'=4,'types_1'=8,'types_2'=4,'tm'=2] {'types_0','types_1','t..., dimensions={0}, use_global_device_ids=true | all-gather | bytes 52428 | tf_op jit(solution)/shard_map/all_gather | solution.py:28
  965.2 9.0 psum.60
  974.3 10.7 %psum.61 = f32[8]{0:T(128)S(1)} all-reduce(f32[8]{0:T(128)S(1)} %psum.60), channel_id=1, replica_groups=mesh['types_0'=4,'types_1'=8,'types_2'=4,'tm'=2] {'types_1'}, use_global_device_ids=true, to_apply=%region_35.36 | all-reduce | flops 8 | bytes 64 | tf_op jit(solution)/shard_map/psum | solution.py:36
  985.0 8.6 psum.62
  995.4 10.1 psum.63
  (3686 shorter events, 868.7 us)
Async XLA Ops:
  0.6 474.4 %copy-start = (f32[8,8]{1,0:T(8,128)S(1)}, f32[8,8]{1,0:T(8,128)}, u32[]{:S(2)}) copy-start(f32[8,8]{1,0:T(8,128)} %param.46) | copy-start | bytes 772
  0.6 13.7 %all-to-all-start = ((s32[6,4,7,512]{3,1,2,0:T(4,128)}), s32[6,4,7,512]{3,1,2,0:T(4,128)S(1)}, u32[]{:S(2)}, u32[]{:S(2)}) async-start(s32[6,4,7,512]{3,1,2,0:T(4,128)} %param.36), calls=%async_computation | async-start | bytes 688128 | tf_op jit(solution)/shard_map/all_to_all | solution.py:157
  7.3 0.7 copy-start.5
  8.0 0.7 copy-start.8
  10.7 0.7 copy-start.4
  11.5 0.7 copy-start.3
  12.9 0.7 copy-start.2
  13.6 0.7 copy-start.7
  14.7 0.7 copy-start.6
  15.4 214.4 %copy-start.1 = (f32[6,7,512]{2,1,0:T(8,128)S(1)}, f32[6,7,512]{2,1,0:T(8,128)}, u32[]{:S(2)}) copy-start(f32[6,7,512]{2,1,0:T(8,128)} %param.38) | copy-start | bytes 258052
  465.1 9.9 copy-start.9
  1005.4 0.5 copy-start.10
where the time goes:
time: 1010 us
  loops' own time  352 us (35%)
  matrix products  238 us (24%)
  other arithmetic  149 us (15%)
  blocking collectives  136 us (13%)
  local copies, waits for them, and re-layouts  121 us (12%)
    another operation x48, loops' own time, forward_period(): lax.fori_loop(0, blocks, forward_block_rows, jnp.zeros_like(weights))  167 us
    another operation x48, loops' own time, backward_period(): lax.fori_loop(0, blocks, backward_block_rows, (zeros_rows, zeros_rows, on...  147 us
    dot_general x192, matrix products, backward_block_rows(): jnp.einsum('eia,cea->cei', onehot, stacked_window, precision=highest)  107 us
    dot_general x192, matrix products, forward_block_rows(): contrib = jnp.einsum('eia,cei->cea', onehot, weight_rows, precision=highest)  79.8 us
    psum x8, blocking collectives, over_axes(): return functools.reduce(lax.psum, axes, array)  73.6 us
    broadcast_in_dim x48, other arithmetic, forward_type(): lax.scan(forward_period, mass_start, (bracket, weight_up, savings, spendi...  64 us
    all_gather x1, blocking collectives, sent_together(): whole = lax.all_gather(both, axis, axis=dim, tiled=True)  62.6 us
    dynamic_update_slice x192, local copies, waits for them, and re-layouts, forward_block_rows(): lax.dynamic_update_slice_in_dim(shifted_mass, current + contrib, window, 2)  49.2 us
  transfers between devices with their start and end apart: 1, of which 0 were waited for; matrix products, arithmetic and copies ran while one was open for 0% of the time, Pallas kernels for 0%

commit v1 on v0

v1 whole, which is shorter than its diff:
```python
import functools

import jax
import jax.numpy as jnp
from jax import lax
from jax.experimental import pallas as pl
from jax.experimental.pallas import tpu as pltpu
from jax.sharding import Mesh
from jax.sharding import PartitionSpec as P

ASSETS = 512
INCOME = 7
BLOCK = 128
REACH = 8
PERIODS = 8
HALF = PERIODS // 2
BLOCKS = ASSETS // BLOCK
ROWS = 16
TYPES = ("types_0", "types_1", "types_2")
EVERY = ("types_0", "types_1", "types_2", "tm")

grid_top = 40.0
grid_scale = grid_top / (ASSETS - 1) ** 2
rate_floor = 0.005
rate_span = 0.03

VMEM = pl.BlockSpec(memory_space=pltpu.VMEM)
SMEM = pl.BlockSpec(memory_space=pltpu.SMEM)


def iota(dim, shape=(ROWS, BLOCK)):
    return lax.broadcasted_iota(jnp.int32, shape, dim)


def by_type(scalars):
    kind = iota(0) // BLOCKS
    value = jnp.full((ROWS, BLOCK), scalars[-1], jnp.float32)
    for k in range(len(scalars) - 2, -1, -1):
        value = jnp.where(kind == k, scalars[k], value)
    return value


def diagonal():
    return iota(0, (PERIODS, PERIODS)) == iota(1, (PERIODS, PERIODS))


def gap_row(totals_row, supply_row, all_types):
    return totals_row * (1.0 / all_types) - supply_row


def price_column(price_row, jac, gaps):
    wide = jnp.where(diagonal(), jnp.broadcast_to(price_row, (PERIODS, PERIODS)), 0.0)
    for gap in gaps:
        wide = wide - jac * gap
    return jnp.sum(wide, axis=1, keepdims=True)


def set_rates(price, rates):
    rate = rate_floor + rate_span / (1.0 + jnp.exp(-price))
    rate = jnp.broadcast_to(rate, (PERIODS, BLOCK))
    rates[0] = rate
    rates[1] = 1.0 / (1.0 + rate)


def solve(core, half_types, patience, productivity, levels, transition, wage, brackets, start, rates, weights, savings, series, full):
    lane, row = iota(1), iota(0)
    point = (row % BLOCKS) * BLOCK + lane
    first = (row % BLOCKS) * BLOCK
    grid = point.astype(jnp.float32)
    grid = grid_scale * grid * grid
    types = [core * half_types + k for k in range(half_types)]
    beta = by_type([patience[k] for k in types])
    skill = by_type([productivity[k] for k in types])
    mixing = [[transition[e, f] for f in range(INCOME)] for e in range(INCOME)]
    pay = [levels[e] for e in range(INCOME)]

    def rate_at(t):
        rate = jnp.broadcast_to(rates[0, pl.ds(t, 1), :], (ROWS, BLOCK))
        inverse = jnp.broadcast_to(rates[1, pl.ds(t, 1), :], (ROWS, BLOCK))
        return rate, inverse

    last, _ = rate_at(PERIODS - 1)
    values = tuple((1.0 + last) / (last * grid + (wage[PERIODS - 1] * pay[e]) * skill) for e in range(INCOME))

    def backward(step, values):
        t = PERIODS - 1 - step
        rate, inverse = rate_at(t)
        budget = (1.0 + rate) * grid
        fresh = []
        for e in range(INCOME):
            mixed = mixing[e][0] * values[0]
            for f in range(1, INCOME):
                mixed = mixed + mixing[e][f] * values[f]
            income = (wage[t] * pay[e]) * skill
            edge = (1.0 / (beta * mixed) + grid - income) * inverse
            above = pltpu.roll(edge, 1, 0)
            bracket = brackets[t, e]
            spot, after = bracket & (BLOCK - 1), (bracket + 1) & (BLOCK - 1)
            lower = jnp.where(
                bracket >= first,
                jnp.take_along_axis(edge, spot, axis=1),
                jnp.take_along_axis(above, spot, axis=1),
            )
            upper = jnp.where(
                bracket + 1 >= first,
                jnp.take_along_axis(edge, after, axis=1),
                jnp.take_along_axis(above, after, axis=1),
            )
            place = bracket.astype(jnp.float32)
            low = grid_scale * place * place
            width = grid_scale * (2.0 * place + 1.0)
            spacing = jnp.maximum(upper - lower, width * inverse)
            weight = jnp.clip((grid - lower) / spacing, 0.0, 1.0)
            saved = low + weight * width
            weights[t, e] = weight
            savings[t, e] = saved
            fresh.append((1.0 + rate) / (budget + income - saved))
        return tuple(fresh)

    lax.fori_loop(0, PERIODS, backward, values)

    def sums(t, masses):
        rate, _ = rate_at(t)
        budget = (1.0 + rate) * grid
        assets = jnp.zeros((ROWS, BLOCK), jnp.float32)
        spent = jnp.zeros((ROWS, BLOCK), jnp.float32)
        for e in range(INCOME):
            saved = savings[t, e]
            assets = assets + masses[e] * saved
            if full:
                spent = spent + masses[e] * (budget + (wage[t] * pay[e]) * skill - saved)
        series[0, t] = assets
        if full:
            series[1, t] = spent

    def forward(t, masses):
        sums(t, masses)
        arrived = []
        for e in range(INCOME):
            weight = weights[t, e]
            rising = weight * masses[e]
            staying = (1.0 - weight) * masses[e]
            drop = point - brackets[t, e]
            hit = [drop == s for s in range(REACH + 2)]
            here = jnp.where(hit[0], staying, jnp.where(hit[1], rising, 0.0))
            here = here + pltpu.roll(jnp.where(hit[0], rising, 0.0), 1, 1)
            crossed = jnp.zeros((ROWS, BLOCK), jnp.float32)
            for s in range(1, REACH + 2):
                moved = jnp.where(hit[s], staying, jnp.where(hit[s + 1], rising, 0.0) if s <= REACH else 0.0)
                moved = pltpu.roll(moved, BLOCK - s, 1)
                inside = lane < BLOCK - s
                here = here + jnp.where(inside, moved, 0.0)
                crossed = crossed + jnp.where(inside, 0.0, moved)
            arrived.append(here + pltpu.roll(crossed, ROWS - 1, 0))
        fresh = []
        for f in range(INCOME):
            mixed = mixing[0][f] * arrived[0]
            for e in range(1, INCOME):
                mixed = mixed + mixing[e][f] * arrived[e]
            fresh.append(mixed)
        return tuple(fresh)

    masses = tuple(start[e] for e in range(INCOME))
    masses = lax.fori_loop(0, PERIODS - 1, forward, masses)
    sums(PERIODS - 1, masses)


def lane_sums(arrays):
    lane = iota(1)
    held = jnp.zeros((ROWS, BLOCK), jnp.float32)
    for q, array in enumerate(arrays):
        held = jnp.where(lane == q, jnp.sum(array, axis=1, keepdims=True), held)
    return held


def first_kernel(
    blocks, patience, productivity, levels, transition, wage, split, mass, price,
    out, brackets, start, rates, weights, savings, series,
):
    half_types = split.shape[1]
    core = lax.axis_index("tm")
    for k in range(half_types):
        alive = blocks[core * half_types + k]
        for e in range(INCOME):
            for b in range(BLOCKS):
                line = pl.ds(k * BLOCKS + b, 1)
                part = pl.ds(b * BLOCK, BLOCK)
                live = (b < alive).astype(jnp.float32)
                start[e, line, :] = mass[core * half_types + k, pl.ds(e, 1), part] * live
                for t in range(PERIODS):
                    brackets[t, e, line, :] = split[t // HALF, k, e, pl.ds(t % HALF, 1), part]
    spare = ROWS - half_types * BLOCKS
    for e in range(INCOME):
        start[e, ROWS - spare :, :] = jnp.zeros((spare, BLOCK), jnp.float32)
        for t in range(PERIODS):
            brackets[t, e, ROWS - spare :, :] = brackets[t, e, ROWS - 2 * spare : ROWS - spare, :]
    set_rates(price_column(price[...], None, ()), rates)
    solve(core, half_types, patience, productivity, levels, transition, wage, brackets, start, rates, weights, savings, series, False)
    held = lane_sums([series[0, t] for t in range(PERIODS)])
    total = jnp.sum(held, axis=0, keepdims=True)[:, :PERIODS]
    out[...] = jnp.broadcast_to(total, out.shape)


def second_kernel(
    patience, productivity, levels, transition, wage, brackets, start, price, jac, supply, totals,
    out, gap_out, rates, weights, savings, series,
    *, half_types, all_types,
):
    core = lax.axis_index("tm")
    total = jnp.sum(totals[...], axis=0, keepdims=True)
    gap = gap_row(total, supply[...], all_types)
    gap_out[...] = gap
    set_rates(price_column(price[...], jac[...], (gap,)), rates)
    solve(core, half_types, patience, productivity, levels, transition, wage, brackets, start, rates, weights, savings, series, True)
    held = lane_sums([series[c, t] for c in range(2) for t in range(PERIODS)])
    for k in range(half_types):
        line = jnp.sum(held[k * BLOCKS : (k + 1) * BLOCKS], axis=0, keepdims=True)
        width = 2 * PERIODS
        out[:, k * width : (k + 1) * width] = jnp.broadcast_to(line[:, :width], (out.shape[0], width))


def last_kernel(assignment, price, jac, supply, first_gap, everything, price_out, gap_out, paths_out, *, half_types, all_types):
    here = lax.axis_index(TYPES)
    width = 2 * PERIODS
    total = jnp.sum(everything[...], axis=0, keepdims=True)
    assets = total[:, :PERIODS]
    for k in range(1, half_types):
        assets = assets + total[:, k * width : k * width + PERIODS]
    gap = gap_row(assets, supply[...], all_types)
    gap_out[...] = gap
    column = price_column(price[...], jac[...], (first_gap[...], gap))
    price_out[...] = jnp.sum(jnp.where(diagonal(), column, 0.0), axis=0, keepdims=True)
    slots = paths_out.shape[0]
    for s in range(slots):
        wanted = assignment[here * slots + s]
        line = everything[pl.ds(wanted // half_types, 1), :]
        kind = wanted % half_types
        found = line[:, :width]
        for k in range(1, half_types):
            found = jnp.where(kind == k, line[:, k * width : (k + 1) * width], found)
        for c in range(2):
            paths_out[s, pl.ds(c, 1), :] = found[:, c * PERIODS : (c + 1) * PERIODS]


def body(
    brackets,
    active_blocks,
    initial_mass,
    patience,
    productivity,
    income_levels,
    income_transition,
    wage_path,
    bond_supply,
    price_guess,
    jac_inverse,
    assignment,
):
    local_types = patience.shape[0]
    all_types = local_types * lax.axis_size(TYPES)
    cores = lax.axis_size("tm")
    devices = lax.axis_size(EVERY)
    half_types = local_types // cores
    f32, i32 = jnp.float32, jnp.int32
    shape = jax.ShapeDtypeStruct
    by_income = jnp.transpose(brackets, (0, 2, 1, 3)).reshape(cores, half_types, INCOME, HALF, ASSETS)
    split = lax.all_to_all(by_income, "tm", split_axis=0, concat_axis=0, tiled=True)
    price_row = price_guess.reshape(1, PERIODS)
    supply_row = bond_supply.reshape(1, PERIODS)
    work = [
        pltpu.VMEM((2, PERIODS, BLOCK), f32),
        pltpu.VMEM((PERIODS, INCOME, ROWS, BLOCK), f32),
        pltpu.VMEM((PERIODS, INCOME, ROWS, BLOCK), f32),
        pltpu.VMEM((2, PERIODS, ROWS, BLOCK), f32),
    ]
    sent, by_row, start = pl.pallas_call(
        first_kernel,
        name="first_round",
        out_shape=(
            shape((devices, PERIODS), f32),
            shape((PERIODS, INCOME, ROWS, BLOCK), i32),
            shape((INCOME, ROWS, BLOCK), f32),
        ),
        in_specs=[SMEM] * 6 + [VMEM] * 3,
        out_specs=(VMEM,) * 3,
        scratch_shapes=work,
    )(active_blocks, patience, productivity, income_levels, income_transition, wage_path, split, initial_mass, price_row)
    totals = lax.all_to_all(sent, EVERY, split_axis=0, concat_axis=0, tiled=True)
    sent, first_gap = pl.pallas_call(
        functools.partial(second_kernel, half_types=half_types, all_types=all_types),
        name="second_round",
        out_shape=(shape((devices, half_types * 2 * PERIODS), f32), shape((1, PERIODS), f32)),
        in_specs=[SMEM] * 5 + [VMEM] * 6,
        out_specs=(VMEM,) * 2,
        scratch_shapes=work,
    )(patience, productivity, income_levels, income_transition, wage_path, by_row, start, price_row, jac_inverse, supply_row, totals)
    everything = lax.all_to_all(sent, EVERY, split_axis=0, concat_axis=0, tiled=True)
    price_path, market_gap, type_paths = pl.pallas_call(
        functools.partial(last_kernel, half_types=half_types, all_types=all_types),
        name="last_update",
        out_shape=(shape((1, PERIODS), f32), shape((1, PERIODS), f32), shape((local_types, 2, PERIODS), f32)),
        in_specs=[SMEM] + [VMEM] * 5,
        out_specs=(VMEM,) * 3,
    )(assignment, price_row, jac_inverse, supply_row, first_gap, everything)
    return price_path.reshape(PERIODS), market_gap.reshape(PERIODS), type_paths


def solution(mesh):
    torus = Mesh(
        mesh.devices.reshape(4, 8, 4, mesh.shape["tm"]), ("types_0", "types_1", "types_2", "tm")
    )
    in_specs = (
        P(TYPES, "tm", None, None),
        P(TYPES),
        P(TYPES, None, None),
        P(TYPES),
        P(TYPES),
        P(),
        P(),
        P(),
        P(),
        P(),
        P(),
        P(),
    )
    out_specs = (P(), P(), P(TYPES, None, None))
    return jax.shard_map(body, mesh=torus, in_specs=in_specs, out_specs=out_specs, check_vma=False)
```

time: 1010 us -> 69 us (0.07)
  loops' own time: 352 us -> 0 us
  matrix products: 238 us -> 0 us
  other arithmetic: 149 us -> 0 us
  local copies, waits for them, and re-layouts: 121 us -> 0 us
  blocking collectives: 136 us -> 54.6 us
  Pallas kernels: 0 us -> 13.4 us
    another operation x112 -> x0, loops' own time: 352 us -> none  [the longest x48 167 us: forward_period(): lax.fori_loop(0, blocks, forward_block_rows, jnp.zeros_like(weights))]
    dot_general x483 -> x0, matrix products: 238 us -> none  [the longest x192 107 us: backward_block_rows(): jnp.einsum('eia,cea->cei', onehot, stacked_window, precision=highest)]
    psum x8 -> x0, blocking collectives: 73.6 us -> none  [over_axes(): return functools.reduce(lax.psum, axes, array)]
    broadcast_in_dim x48 -> x0, other arithmetic: 64 us -> none  [forward_type(): lax.scan(forward_period, mass_start, (bracket, weight_up, savings, spendi...]
    all_gather x1 -> x0, blocking collectives: 62.6 us -> none  [sent_together(): whole = lax.all_gather(both, axis, axis=dim, tiled=True)]
    all_to_all x0 -> x3, blocking collectives: none -> 54.6 us  [the longest x2 45.9 us: body(): lax.all_to_all(sent, EVERY, split_axis=0, concat_axis=0, tiled=True)]
    dynamic_update_slice x354 -> x0, local copies, waits for them, and re-layouts: 51.7 us -> none  [the longest x192 49.2 us: forward_block_rows(): lax.dynamic_update_slice_in_dim(shifted_mass, current + contrib, window, 2)]
    dynamic_slice x451 -> x0, local copies, waits for them, and re-layouts: 43.9 us -> none  [the longest x48 29.6 us: backward_type(): lax.scan(backward_period, values_end, (bracket, interest_path, incomes),...]
  transfers between devices with their start and end apart: 1 -> 0, of which waited for: 0 -> 0; matrix products, arithmetic and copies ran while one was open for 0% -> 0% of each run, Pallas kernels for 0% -> 0%
where the time goes in v1:
time: 69 us; the launch traced here: 68.7 us
  blocking collectives  54.6 us (79%)
  Pallas kernels  13.4 us (19%)
    all_to_all x2, blocking collectives, body(): lax.all_to_all(sent, EVERY, split_axis=0, concat_axis=0, tiled=True)  45.9 us
    all_to_all x1, blocking collectives, body(): lax.all_to_all(by_income, 'tm', split_axis=0, concat_axis=0, tiled=True)  8.75 us
    pallas_call x1, Pallas kernels, body(): pl.pallas_call(first_kernel, name='first_round', out_shape=(shape((device...  5.84 us
    pallas_call x1, Pallas kernels, body(): pl.pallas_call(functools.partial(second_kernel, half_types=half_types, al...  5.77 us
    pallas_call x1, Pallas kernels, body(): pl.pallas_call(functools.partial(last_kernel, half_types=half_types, all_...  1.82 us

profile of v1, /device:TPU:1, one launch (start us, length us, event | category | flops | bytes accessed | tf_op | source)
XLA Modules:
  0.0 68.7 jit_solution(8705813838537612440)
XLA Ops:
  0.6 8.8 %all_to_all.27.split = s32[2,3,7,4,512]{4,3,2,1,0:T(4,128)} all-to-all(s32[2,3,7,4,512]{4,3,2,1,0:T(4,128)} %bitcast.17), channel_id=1, replica_groups=mesh['types_0'=4,'types_1'=8,'types_2'=4,'tm'=2] {'tm'}, dimensions={0} | all-to-all | bytes 688128 | tf_op jit(solution)/shard_map/all_to_all | solution.py:267
  9.4 5.8 %first_round.1 = (f32[256,8]{1,0:T(8,128)}, s32[8,7,16,128]{3,2,1,0:T(8,128)}, f32[7,16,128]{2,1,0:T(8,128)}) custom-call(s32[6]{0:T(128)} %blocks.1, f32[6]{0:T(128)} %patience.3, f32[6]{0:T(128)} %productivity.3, f32[7]{0:T(128)} %levels.3, f32[7,7]{1,0:T(8,128)} %transition.3, f32[8]{0:T(128)} %wage.3, s32[2,3,7,4,512]{4,3,2,1,0:T(4,128)} %all_to_all.27.split, ...), custom_call_target="tpu_custom_call" | custom-call | tf_op jit(solution)/shard_map/first_round/pallas_call | solution.py:276
  15.2 25.9 %all_to_all.28 = f32[256,1,8]{2,1,0:T(1,128)} all-to-all(f32[256,1,8]{2,1,0:T(1,128)} %bitcast.19), channel_id=1, replica_groups=mesh['types_0'=4,'types_1'=8,'types_2'=4,'tm'=2] {'types_0','types_1','t..., dimensions={0} | all-to-all | bytes 16384 | tf_op jit(solution)/shard_map/all_to_all | solution.py:288
  41.1 5.8 %second_round.1 = (f32[256,48]{1,0:T(8,128)}, f32[1,8]{1,0:T(1,128)}) custom-call(f32[6]{0:T(128)} %patience.3, f32[6]{0:T(128)} %productivity.3, f32[7]{0:T(128)} %levels.3, f32[7,7]{1,0:T(8,128)} %transition.3, f32[8]{0:T(128)} %wage.3, s32[8,7,16,128]{3,2,1,0:T(8,128)} %get-tuple-element.11.brackets, f32[7,16,128]{2,1,0:T(8,128)} %get-tuple-element.12.start, ...), custom_call_target="tpu_custom_call" | custom-call | tf_op jit(solution)/shard_map/second_round/pallas_call | solution.py:289
  46.9 20.0 %all_to_all.29 = f32[256,1,48]{2,1,0:T(1,128)} all-to-all(f32[256,1,48]{2,1,0:T(1,128)} %bitcast.18), channel_id=1, replica_groups=mesh['types_0'=4,'types_1'=8,'types_2'=4,'tm'=2] {'types_0','types_1','t..., dimensions={0} | all-to-all | bytes 98304 | tf_op jit(solution)/shard_map/all_to_all | solution.py:297
  66.9 1.8 %last_update.1 = (f32[1,8]{1,0:T(1,128)}, f32[1,8]{1,0:T(1,128)}, f32[6,2,8]{2,1,0:T(2,128)}) custom-call(s32[768]{0:T(1024)} %assignment.1, f32[1,8]{1,0:T(1,128)} %bitcast.22, f32[8,8]{1,0:T(8,128)} %jac.3, f32[1,8]{1,0:T(1,128)} %bitcast.24, f32[1,8]{1,0:T(1,128)} %get-tuple-element.14.first_gap, f32[256,48]{1,0:T(8,128)} %bitcast.16), custom_call_target="tpu_custom_call" | custom-call | tf_op jit(solution)/shard_map/last_update/pallas_call | solution.py:298

commit v2 on v1

--- a/solution.py
+++ b/solution.py
@@ -26,6 +26,10 @@
 
 VMEM = pl.BlockSpec(memory_space=pltpu.VMEM)
 SMEM = pl.BlockSpec(memory_space=pltpu.SMEM)
+
+
+def near(array):
+    return pltpu.with_memory_space_constraint(array, pltpu.VMEM)
 
 
 def iota(dim, shape=(ROWS, BLOCK)):
@@ -174,10 +178,10 @@
 
 
 def first_kernel(
-    blocks, patience, productivity, levels, transition, wage, split, mass, price,
+    blocks, patience, productivity, levels, transition, wage, mine, theirs, mass, price,
     out, brackets, start, rates, weights, savings, series,
 ):
-    half_types = split.shape[1]
+    half_types = mine.shape[1]
     core = lax.axis_index("tm")
     for k in range(half_types):
         alive = blocks[core * half_types + k]
@@ -187,8 +191,9 @@
                 part = pl.ds(b * BLOCK, BLOCK)
                 live = (b < alive).astype(jnp.float32)
                 start[e, line, :] = mass[core * half_types + k, pl.ds(e, 1), part] * live
-                for t in range(PERIODS):
-                    brackets[t, e, line, :] = split[t // HALF, k, e, pl.ds(t % HALF, 1), part]
+                for t in range(HALF):
+                    brackets[core * HALF + t, e, line, :] = mine[core, k, e, pl.ds(t, 1), part]
+                    brackets[(1 - core) * HALF + t, e, line, :] = theirs[core, k, e, pl.ds(t, 1), part]
     spare = ROWS - half_types * BLOCKS
     for e in range(INCOME):
         start[e, ROWS - spare :, :] = jnp.zeros((spare, BLOCK), jnp.float32)
@@ -198,7 +203,7 @@
     solve(core, half_types, patience, productivity, levels, transition, wage, brackets, start, rates, weights, savings, series, False)
     held = lane_sums([series[0, t] for t in range(PERIODS)])
     total = jnp.sum(held, axis=0, keepdims=True)[:, :PERIODS]
-    out[...] = jnp.broadcast_to(total, out.shape)
+    out[...] = total
 
 
 def second_kernel(
@@ -216,7 +221,7 @@
     for k in range(half_types):
         line = jnp.sum(held[k * BLOCKS : (k + 1) * BLOCKS], axis=0, keepdims=True)
         width = 2 * PERIODS
-        out[:, k * width : (k + 1) * width] = jnp.broadcast_to(line[:, :width], (out.shape[0], width))
+        out[:, k * width : (k + 1) * width] = line[:, :width]
 
 
 def last_kernel(assignment, price, jac, supply, first_gap, everything, price_out, gap_out, paths_out, *, half_types, all_types):
@@ -264,7 +269,13 @@
     f32, i32 = jnp.float32, jnp.int32
     shape = jax.ShapeDtypeStruct
     by_income = jnp.transpose(brackets, (0, 2, 1, 3)).reshape(cores, half_types, INCOME, HALF, ASSETS)
-    split = lax.all_to_all(by_income, "tm", split_axis=0, concat_axis=0, tiled=True)
+    theirs = lax.ppermute(by_income, "tm", [(c, cores - 1 - c) for c in range(cores)])
+    theirs = near(theirs)
+
+    def exchanged(line):
+        copies = jnp.broadcast_to(line[None], (devices, 1, line.shape[1]))
+        return lax.all_to_all(copies, EVERY, split_axis=0, concat_axis=0, tiled=True).reshape(devices, -1)
+
     price_row = price_guess.reshape(1, PERIODS)
     supply_row = bond_supply.reshape(1, PERIODS)
     work = [
@@ -277,31 +288,31 @@
         first_kernel,
         name="first_round",
         out_shape=(
-            shape((devices, PERIODS), f32),
-            shape((PERIODS, INCOME, ROWS, BLOCK), i32),
-            shape((INCOME, ROWS, BLOCK), f32),
+            pltpu.VMEM((1, PERIODS), f32),
+            pltpu.VMEM((PERIODS, INCOME, ROWS, BLOCK), i32),
+            pltpu.VMEM((INCOME, ROWS, BLOCK), f32),
         ),
-        in_specs=[SMEM] * 6 + [VMEM] * 3,
+        in_specs=[SMEM] * 6 + [VMEM] * 4,
         out_specs=(VMEM,) * 3,
         scratch_shapes=work,
-    )(active_blocks, patience, productivity, income_levels, income_transition, wage_path, split, initial_mass, price_row)
-    totals = lax.all_to_all(sent, EVERY, split_axis=0, concat_axis=0, tiled=True)
+    )(active_blocks, patience, productivity, income_levels, income_transition, wage_path, by_income, theirs, initial_mass, price_row)
+    totals = near(exchanged(sent))
     sent, first_gap = pl.pallas_call(
         functools.partial(second_kernel, half_types=half_types, all_types=all_types),
         name="second_round",
-        out_shape=(shape((devices, half_types * 2 * PERIODS), f32), shape((1, PERIODS), f32)),
+        out_shape=(pltpu.VMEM((1, half_types * 2 * PERIODS), f32), pltpu.VMEM((1, PERIODS), f32)),
         in_specs=[SMEM] * 5 + [VMEM] * 6,
         out_specs=(VMEM,) * 2,
         scratch_shapes=work,
-    )(patience, productivity, income_levels, income_transition, wage_path, by_row, start, price_row, jac_inverse, supply_row, totals)
-    everything = lax.all_to_all(sent, EVERY, split_axis=0, concat_axis=0, tiled=True)
+    )(patience, productivity, income_levels, income_transition, wage_path, near(by_row), near(start), price_row, jac_inverse, supply_row, totals)
+    everything = near(exchanged(sent))
     price_path, market_gap, type_paths = pl.pallas_call(
         functools.partial(last_kernel, half_types=half_types, all_types=all_types),
         name="last_update",
         out_shape=(shape((1, PERIODS), f32), shape((1, PERIODS), f32), shape((local_types, 2, PERIODS), f32)),
         in_specs=[SMEM] + [VMEM] * 5,
         out_specs=(VMEM,) * 3,
-    )(assignment, price_row, jac_inverse, supply_row, first_gap, everything)
+    )(assignment, price_row, jac_inverse, supply_row, near(first_gap), everything)
     return price_path.reshape(PERIODS), market_gap.reshape(PERIODS), type_paths
 
 

time: 69 us -> 61.1 us (0.89)
  blocking collectives: 54.6 us -> 43.6 us
  starting transfers between devices: 0 us -> 3.33 us
  Pallas kernels: 13.4 us -> 11.7 us
  waiting for transfers between devices: 0 us -> 1.49 us
    all_to_all x3 -> x2, blocking collectives: 54.6 us -> 43.6 us  [exchanged(): lax.all_to_all(copies, EVERY, split_axis=0, concat_axis=0, tiled=True)]
    ppermute x0 -> x1, starting transfers between devices: none -> 3.33 us  [body(): lax.ppermute(by_income, 'tm', [(c, cores - 1 - c) for c in range(cores)])]
    ppermute x0 -> x1, waiting for transfers between devices: none -> 1.49 us  [body(): lax.ppermute(by_income, 'tm', [(c, cores - 1 - c) for c in range(cores)])]
    pallas_call x1, Pallas kernels: 5.77 us -> 4.87 us  [body(): pl.pallas_call(functools.partial(second_kernel, half_types=half_types, al...]
    pallas_call x1, Pallas kernels: 5.84 us -> 5.11 us  [body(): pl.pallas_call(first_kernel, name='first_round', out_shape=(pltpu.VMEM((1...]
  transfers between devices with their start and end apart: 0 -> 1, of which waited for: 0 -> 1; matrix products, arithmetic and copies ran while one was open for 0% -> 0% of each run, Pallas kernels for 0% -> 0%
where the time goes in v2:
time: 61.1 us; the launch traced here: 60.9 us
  blocking collectives  43.6 us (71%)
  Pallas kernels  11.7 us (19%)
  starting transfers between devices  3.33 us (5%)
  waiting for transfers between devices  1.49 us (2%)
  between operations  0.65 us (1%)
    all_to_all x2, blocking collectives, exchanged(): lax.all_to_all(copies, EVERY, split_axis=0, concat_axis=0, tiled=True)  43.6 us
    pallas_call x1, Pallas kernels, body(): pl.pallas_call(first_kernel, name='first_round', out_shape=(pltpu.VMEM((1...  5.11 us
    pallas_call x1, Pallas kernels, body(): pl.pallas_call(functools.partial(second_kernel, half_types=half_types, al...  4.87 us
    ppermute x1, starting transfers between devices, body(): lax.ppermute(by_income, 'tm', [(c, cores - 1 - c) for c in range(cores)])  3.33 us
    pallas_call x1, Pallas kernels, body(): pl.pallas_call(functools.partial(last_kernel, half_types=half_types, all_...  1.69 us
    ppermute x1, waiting for transfers between devices, body(): lax.ppermute(by_income, 'tm', [(c, cores - 1 - c) for c in range(cores)])  1.49 us
  transfers between devices with their start and end apart: 1, of which 1 were waited for; matrix products, arithmetic and copies ran while one was open for 0% of the time, Pallas kernels for 0%

profile of v2, /device:TPU:1, one launch (start us, length us, event | category | flops | bytes accessed | tf_op | source)
XLA Modules:
  0.0 60.9 jit_solution(13809094962209422969)
XLA Ops:
  0.6 3.3 %collective-permute-start = (s32[2,3,7,4,512]{4,3,2,1,0:T(4,128)}, s32[2,3,7,4,512]{4,3,2,1,0:T(4,128)S(1)}, u32[]{:S(2)}, u32[]{:S(2)}) collective-permute-start(s32[2,3,7,4,512]{4,3,2,1,0:T(4,128)} %bitcast.15), channel_id=1, source_target_pairs={{0,1},{1,0},{2,3},{3,2},{4,5},{5,4},{6,7},{7,6},{8,9},{9,8},{10,11... | collective-permute-start | bytes 1032200 | tf_op jit(solution)/shard_map/ppermute | solution.py:272
  4.0 1.5 %collective-permute-done.theirs = s32[2,3,7,4,512]{4,3,2,1,0:T(4,128)S(1)} collective-permute-done((s32[2,3,7,4,512]{4,3,2,1,0:T(4,128)}, s32[2,3,7,4,512]{4,3,2,1,0:T(4,128)S(1)}, u32[]{:S(2)}, u32[]{:S(2)}) %collective-permute-start) | collective-permute-done | bytes 344096 | tf_op jit(solution)/shard_map/ppermute | solution.py:272
  5.4 5.1 %first_round.1 = (f32[1,8]{1,0:T(1,128)S(1)}, s32[8,7,16,128]{3,2,1,0:T(8,128)S(1)}, f32[7,16,128]{2,1,0:T(8,128)S(1)}) custom-call(s32[6]{0:T(128)} %blocks.1, f32[6]{0:T(128)} %patience.3, f32[6]{0:T(128)} %productivity.3, f32[7]{0:T(128)} %levels.3, f32[7,7]{1,0:T(8,128)} %transition.3, f32[8]{0:T(128)} %wage.3, s32[2,3,7,4,512]{4,3,2,1,0:T(4,128)} %bitcast.16, ...), custom_call_target="tpu_custom_call" | custom-call | tf_op jit(solution)/shard_map/first_round/pallas_call | solution.py:287
  10.6 0.1 broadcast_in_dim.17
  10.6 25.5 %all_to_all.10 = f32[256,1,8]{2,1,0:T(1,128)S(1)} all-to-all(f32[256,1,8]{2,1,0:T(1,128)S(1)} %broadcast_in_dim.17), channel_id=1, replica_groups=mesh['types_0'=4,'types_1'=8,'types_2'=4,'tm'=2] {'types_0','types_1','t..., dimensions={0} | all-to-all | bytes 16384 | tf_op jit(solution)/shard_map/all_to_all | solution.py:277
  36.1 4.9 %second_round.1 = (f32[1,48]{1,0:T(1,128)S(1)}, f32[1,8]{1,0:T(1,128)S(1)}) custom-call(f32[6]{0:T(128)} %patience.3, f32[6]{0:T(128)} %productivity.3, f32[7]{0:T(128)} %levels.3, f32[7,7]{1,0:T(8,128)} %transition.3, f32[8]{0:T(128)} %wage.3, s32[8,7,16,128]{3,2,1,0:T(8,128)S(1)} %get-tuple-element.11.brackets, f32[7,16,128]{2,1,0:T(8,128)S(1)} %get-tuple-element.12.start, ...), custom_call_target="tpu_custom_call" | custom-call | tf_op jit(solution)/shard_map/second_round/pallas_call | solution.py:300
  41.0 0.1 broadcast_in_dim.19
  41.1 18.2 %all_to_all.11 = f32[256,1,48]{2,1,0:T(1,128)S(1)} all-to-all(f32[256,1,48]{2,1,0:T(1,128)S(1)} %broadcast_in_dim.19), channel_id=1, replica_groups=mesh['types_0'=4,'types_1'=8,'types_2'=4,'tm'=2] {'types_0','types_1','t..., dimensions={0} | all-to-all | bytes 98304 | tf_op jit(solution)/shard_map/all_to_all | solution.py:277
  59.2 1.7 %last_update.1 = (f32[1,8]{1,0:T(1,128)}, f32[1,8]{1,0:T(1,128)}, f32[6,2,8]{2,1,0:T(2,128)}) custom-call(s32[768]{0:T(1024)} %assignment.1, f32[1,8]{1,0:T(1,128)} %bitcast.19, f32[8,8]{1,0:T(8,128)} %jac.3, f32[1,8]{1,0:T(1,128)} %bitcast.21, f32[1,8]{1,0:T(1,128)S(1)} %get-tuple-element.14.first_gap, f32[256,48]{1,0:T(8,128)S(1)} %bitcast.12), custom_call_target="tpu_custom_call" | custom-call | tf_op jit(solution)/shard_map/last_update/pallas_call | solution.py:309
Async XLA Ops:
  0.6 4.8 %collective-permute-start = (s32[2,3,7,4,512]{4,3,2,1,0:T(4,128)}, s32[2,3,7,4,512]{4,3,2,1,0:T(4,128)S(1)}, u32[]{:S(2)}, u32[]{:S(2)}) collective-permute-start(s32[2,3,7,4,512]{4,3,2,1,0:T(4,128)} %bitcast.15), channel_id=1, source_target_pairs={{0,1},{1,0},{2,3},{3,2},{4,5},{5,4},{6,7},{7,6},{8,9},{9,8},{10,11... | collective-permute-start | bytes 1032200 | tf_op jit(solution)/shard_map/ppermute | solution.py:272

commit v3 on v2

v3 whole, which is shorter than its diff:
```python
import functools

import jax
import jax.numpy as jnp
from jax import lax
from jax.experimental import pallas as pl
from jax.experimental.pallas import tpu as pltpu
from jax.sharding import Mesh
from jax.sharding import PartitionSpec as P

ASSETS = 512
INCOME = 7
BLOCK = 128
REACH = 8
PERIODS = 8
HALF = PERIODS // 2
BLOCKS = ASSETS // BLOCK
TILE = 8
SHARE = 3 * BLOCKS
LINES = INCOME * SHARE
CHUNKS = -(-LINES // TILE)
ROWS = CHUNKS * TILE
DEEP = ROWS + 2 * TILE
WIDE = 2 * TILE
FRAME = 2 * SHARE
WAGE = 56
TYPES = ("types_0", "types_1", "types_2")
EVERY = ("types_0", "types_1", "types_2", "tm")

grid_top = 40.0
grid_scale = grid_top / (ASSETS - 1) ** 2
rate_floor = 0.005
rate_span = 0.03

VMEM = pl.BlockSpec(memory_space=pltpu.VMEM)
SMEM = pl.BlockSpec(memory_space=pltpu.SMEM)


def near(array):
    return pltpu.with_memory_space_constraint(array, pltpu.VMEM)


def iota(dim, shape=(TILE, BLOCK)):
    return lax.broadcasted_iota(jnp.int32, shape, dim)


def rows_of(chunk):
    return pl.ds(chunk * TILE, TILE)


def splat(row, rows=TILE):
    return jnp.broadcast_to(row, (rows, BLOCK))


def diagonal():
    return iota(0, (PERIODS, PERIODS)) == iota(1, (PERIODS, PERIODS))


def gap_row(totals_row, supply_row, all_types):
    return totals_row * (1.0 / all_types) - supply_row


def price_column(price_row, jac, gaps):
    wide = jnp.where(diagonal(), jnp.broadcast_to(price_row, (PERIODS, PERIODS)), 0.0)
    for gap in gaps:
        wide = wide - jac * gap
    return jnp.sum(wide, axis=1, keepdims=True)


def set_rates(price, rates):
    rate = rate_floor + rate_span / (1.0 + jnp.exp(-price))
    rate = jnp.broadcast_to(rate, (PERIODS, BLOCK))
    rates[0] = rate
    rates[1] = 1.0 / (1.0 + rate)


def pattern():
    first = (iota(0) % BLOCKS) * BLOCK
    point = first + iota(1)
    place = point.astype(jnp.float32)
    return point, first, grid_scale * place * place


def mix(source, target, consts, offset, transposed):
    states = [source(e) for e in range(INCOME)]
    for e in range(INCOME):
        total = None
        for f in range(INCOME):
            at = f * INCOME + e if transposed else e * INCOME + f
            term = splat(consts[pl.ds(at, 1), :], WIDE) * states[f]
            total = term if total is None else total + term
        target[pl.ds(offset + e * SHARE, WIDE), :] = total


def solve(consts, beta, pay, brackets, start, rates, weights, savings, values, edges, masses, crossings, series, full):
    point, first, grid = pattern()
    lane = iota(1)

    def rate_at(t):
        return splat(rates[0, pl.ds(t, 1), :]), splat(rates[1, pl.ds(t, 1), :])

    def wage_at(t):
        return splat(consts[pl.ds(WAGE + t, 1), :])

    last, _ = rate_at(PERIODS - 1)
    wage = wage_at(PERIODS - 1)
    for c in range(CHUNKS):
        values[rows_of(c), :] = (1.0 + last) / (last * grid + wage * pay[rows_of(c), :])

    def backward(step, carried):
        t = PERIODS - 1 - step
        rate, inverse = rate_at(t)
        wage = wage_at(t)
        budget = (1.0 + rate) * grid
        mix(lambda e: values[pl.ds(e * SHARE, WIDE), :], edges, consts, TILE, False)
        for c in range(CHUNKS):
            line = pl.ds(TILE + c * TILE, TILE)
            income = wage * pay[rows_of(c), :]
            edges[line, :] = (1.0 / (beta[rows_of(c), :] * edges[line, :]) + grid - income) * inverse
        for c in range(CHUNKS):
            income = wage * pay[rows_of(c), :]
            edge = edges[pl.ds(TILE + c * TILE, TILE), :]
            above = edges[pl.ds(TILE + c * TILE - 1, TILE), :]
            bracket = brackets[t, rows_of(c), :]
            spot, after = bracket & (BLOCK - 1), (bracket + 1) & (BLOCK - 1)
            lower = jnp.where(
                bracket >= first,
                jnp.take_along_axis(edge, spot, axis=1),
                jnp.take_along_axis(above, spot, axis=1),
            )
            upper = jnp.where(
                bracket + 1 >= first,
                jnp.take_along_axis(edge, after, axis=1),
                jnp.take_along_axis(above, after, axis=1),
            )
            place = bracket.astype(jnp.float32)
            low = grid_scale * place * place
            width = grid_scale * (2.0 * place + 1.0)
            spacing = jnp.maximum(upper - lower, width * inverse)
            weight = jnp.clip((grid - lower) / spacing, 0.0, 1.0)
            saved = low + weight * width
            weights[t, rows_of(c), :] = weight
            savings[t, rows_of(c), :] = saved
            values[rows_of(c), :] = (1.0 + rate) / (budget + income - saved)
        return carried

    lax.fori_loop(0, PERIODS, backward, 0)
    for c in range(CHUNKS):
        masses[rows_of(c), :] = start[rows_of(c), :]

    def sums(t):
        rate, _ = rate_at(t)
        wage = wage_at(t)
        budget = (1.0 + rate) * grid
        parts = FRAME // TILE
        assets, spent = [None] * parts, [None] * parts
        for c in range(CHUNKS):
            mass, saved = masses[rows_of(c), :], savings[t, rows_of(c), :]
            terms = [mass * saved]
            if full:
                terms.append(mass * (budget + wage * pay[rows_of(c), :] - saved))
            if (c + 1) * TILE > LINES:
                terms = [jnp.where(iota(0) < LINES - c * TILE, term, 0.0) for term in terms]
            for held, term in zip((assets, spent), terms):
                held[c % parts] = term if held[c % parts] is None else held[c % parts] + term
        for q, held in enumerate((assets, spent) if full else (assets,)):
            for part in range(parts):
                series[q, t, pl.ds(part * TILE, TILE), :] = held[part]

    def forward(t, carried):
        sums(t)
        for c in range(CHUNKS):
            mass, weight = masses[rows_of(c), :], weights[t, rows_of(c), :]
            rising = weight * mass
            staying = (1.0 - weight) * mass
            drop = point - brackets[t, rows_of(c), :]
            hit = [drop == s for s in range(REACH + 2)]
            here = jnp.where(hit[0], staying, jnp.where(hit[1], rising, 0.0))
            here = here + pltpu.roll(jnp.where(hit[0], rising, 0.0), 1, 1)
            crossed = jnp.zeros((TILE, BLOCK), jnp.float32)
            for s in range(1, REACH + 2):
                moved = jnp.where(hit[s], staying, jnp.where(hit[s + 1], rising, 0.0) if s <= REACH else 0.0)
                moved = pltpu.roll(moved, BLOCK - s, 1)
                inside = lane < BLOCK - s
                here = here + jnp.where(inside, moved, 0.0)
                crossed = crossed + jnp.where(inside, 0.0, moved)
            edges[rows_of(c), :] = here
            crossings[rows_of(c), :] = crossed

        def arrived(e):
            return edges[pl.ds(e * SHARE, WIDE), :] + crossings[pl.ds(e * SHARE + 1, WIDE), :]

        mix(arrived, masses, consts, 0, True)
        return carried

    lax.fori_loop(0, PERIODS - 1, forward, 0)
    sums(PERIODS - 1)


def start_kernel(
    blocks, patience, productivity, levels, transition, wage, assignment, mine, mass, price_in, jac_in, supply_in,
    own, start, consts, beta, pay, wanted, price, jac, supply,
):
    price[...], jac[...], supply[...] = price_in[...], jac_in[...], supply_in[...]
    half_types = mine.shape[1]
    core = lax.axis_index("tm")
    here = lax.axis_index(TYPES)
    for e in range(INCOME):
        for f in range(INCOME):
            consts[e * INCOME + f : e * INCOME + f + 1, :] = jnp.full((1, BLOCK), transition[e, f], jnp.float32)
    for t in range(PERIODS):
        consts[WAGE + t : WAGE + t + 1, :] = jnp.full((1, BLOCK), wage[t], jnp.float32)
    for s in range(TILE):
        slot = here * 2 * half_types + min(s, 2 * half_types - 1)
        wanted[s : s + 1, :] = jnp.full((1, BLOCK), assignment[slot], jnp.int32)
    for k in range(half_types):
        alive = blocks[core * half_types + k]
        patient, skill = patience[core * half_types + k], productivity[core * half_types + k]
        for e in range(INCOME):
            top = e * SHARE + k * BLOCKS
            beta[top : top + BLOCKS, :] = jnp.full((BLOCKS, BLOCK), patient, jnp.float32)
            pay[top : top + BLOCKS, :] = jnp.full((BLOCKS, BLOCK), skill * levels[e], jnp.float32)
            for b in range(BLOCKS):
                line, part = pl.ds(top + b, 1), pl.ds(b * BLOCK, BLOCK)
                live = (b < alive).astype(jnp.float32)
                start[line, :] = mass[core * half_types + k, pl.ds(e, 1), part] * live
                for t in range(HALF):
                    own[t, line, :] = mine[core, k, e, pl.ds(t, 1), part]
    spare = ROWS - LINES
    beta[LINES:, :] = jnp.ones((spare, BLOCK), jnp.float32)
    pay[LINES:, :] = jnp.ones((spare, BLOCK), jnp.float32)
    start[LINES:, :] = jnp.zeros((spare, BLOCK), jnp.float32)
    for t in range(HALF):
        own[t, LINES:, :] = jnp.zeros((spare, BLOCK), jnp.int32)


def first_kernel(
    own, theirs, start, consts, beta, pay, price,
    out, brackets, rates, weights, savings, values, edges, masses, crossings, series,
):
    half_types = theirs.shape[1]
    core = lax.axis_index("tm")
    for t in range(HALF):
        brackets[core * HALF + t] = own[t]
        brackets[(1 - core) * HALF + t, LINES:, :] = jnp.zeros((ROWS - LINES, BLOCK), jnp.int32)
    for k in range(half_types):
        for e in range(INCOME):
            for b in range(BLOCKS):
                line, part = pl.ds(e * SHARE + k * BLOCKS + b, 1), pl.ds(b * BLOCK, BLOCK)
                for t in range(HALF):
                    brackets[(1 - core) * HALF + t, line, :] = theirs[core, k, e, pl.ds(t, 1), part]
    set_rates(price_column(price[...], None, ()), rates)
    solve(consts, beta, pay, brackets, start, rates, weights, savings, values, edges, masses, crossings, series, False)
    lane = iota(1)
    held = jnp.zeros((TILE, BLOCK), jnp.float32)
    for t in range(PERIODS):
        total = series[0, t, :TILE, :]
        for part in range(1, FRAME // TILE):
            total = total + series[0, t, part * TILE : (part + 1) * TILE, :]
        held = jnp.where(lane == t, jnp.sum(total, axis=1, keepdims=True), held)
    out[...] = jnp.sum(held, axis=0, keepdims=True)[:, :PERIODS]


def second_kernel(
    brackets, start, consts, beta, pay, price, jac, supply, totals,
    out, gap_out, rates, weights, savings, values, edges, masses, crossings, series,
    *, half_types, all_types,
):
    total = jnp.sum(totals[...], axis=0, keepdims=True)
    gap = gap_row(total, supply[...], all_types)
    gap_out[...] = gap
    set_rates(price_column(price[...], jac[...], (gap,)), rates)
    solve(consts, beta, pay, brackets, start, rates, weights, savings, values, edges, masses, crossings, series, True)
    lane = iota(1, (SHARE, BLOCK))
    held = jnp.zeros((SHARE, BLOCK), jnp.float32)
    width = 2 * PERIODS
    for q in range(width):
        both = series[q // PERIODS, q % PERIODS, :SHARE, :] + series[q // PERIODS, q % PERIODS, SHARE:, :]
        held = jnp.where(lane == q, jnp.sum(both, axis=1, keepdims=True), held)
    for k in range(half_types):
        line = jnp.sum(held[k * BLOCKS : (k + 1) * BLOCKS], axis=0, keepdims=True)
        out[:, k * width : (k + 1) * width] = line[:, :width]


def last_kernel(wanted, price, jac, supply, first_gap, everything, price_out, gap_out, paths_out, *, half_types, all_types):
    width = 2 * PERIODS
    rows = everything.shape[0]
    total = jnp.sum(everything[...], axis=0, keepdims=True)
    assets = total[:, :PERIODS]
    for k in range(1, half_types):
        assets = assets + total[:, k * width : k * width + PERIODS]
    gap = gap_row(assets, supply[...], all_types)
    gap_out[...] = gap
    column = price_column(price[...], jac[...], (first_gap[...], gap))
    price_out[...] = jnp.sum(jnp.where(diagonal(), column, 0.0), axis=0, keepdims=True)
    span = half_types * width
    owner = iota(0, (rows, span)) * half_types + iota(1, (rows, span)) // width
    for s in range(paths_out.shape[0]):
        picked = jnp.where(owner == wanted[pl.ds(s, 1), :span], everything[...], 0.0)
        line = jnp.sum(picked, axis=0, keepdims=True)
        found = line[:, :width]
        for k in range(1, half_types):
            found = found + line[:, k * width : (k + 1) * width]
        for c in range(2):
            paths_out[s, pl.ds(c, 1), :] = found[:, c * PERIODS : (c + 1) * PERIODS]


def body(
    brackets,
    active_blocks,
    initial_mass,
    patience,
    productivity,
    income_levels,
    income_transition,
    wage_path,
    bond_supply,
    price_guess,
    jac_inverse,
    assignment,
):
    local_types = patience.shape[0]
    all_types = local_types * lax.axis_size(TYPES)
    cores = lax.axis_size("tm")
    devices = lax.axis_size(EVERY)
    half_types = local_types // cores
    f32, i32 = jnp.float32, jnp.int32
    by_income = jnp.transpose(brackets, (0, 2, 1, 3)).reshape(cores, half_types, INCOME, HALF, ASSETS)
    theirs = near(lax.ppermute(by_income, "tm", [(c, cores - 1 - c) for c in range(cores)]))

    def exchanged(line):
        copies = jnp.broadcast_to(line[None], (devices, 1, line.shape[1]))
        return near(lax.all_to_all(copies, EVERY, split_axis=0, concat_axis=0, tiled=True).reshape(devices, -1))

    work = [
        pltpu.VMEM((2, PERIODS, BLOCK), f32),
        pltpu.VMEM((PERIODS, ROWS, BLOCK), f32),
        pltpu.VMEM((PERIODS, ROWS, BLOCK), f32),
        pltpu.VMEM((DEEP, BLOCK), f32),
        pltpu.VMEM((DEEP, BLOCK), f32),
        pltpu.VMEM((DEEP, BLOCK), f32),
        pltpu.VMEM((DEEP, BLOCK), f32),
        pltpu.VMEM((2, PERIODS, FRAME, BLOCK), f32),
    ]
    own, *shared, wanted, price_row, jac, supply_row = pl.pallas_call(
        start_kernel,
        name="start",
        out_shape=(
            pltpu.VMEM((HALF, ROWS, BLOCK), i32),
            pltpu.VMEM((ROWS, BLOCK), f32),
            pltpu.VMEM((WAGE + PERIODS, BLOCK), f32),
            pltpu.VMEM((ROWS, BLOCK), f32),
            pltpu.VMEM((ROWS, BLOCK), f32),
            pltpu.VMEM((TILE, BLOCK), i32),
            pltpu.VMEM((1, PERIODS), f32),
            pltpu.VMEM((PERIODS, PERIODS), f32),
            pltpu.VMEM((1, PERIODS), f32),
        ),
        in_specs=[SMEM] * 7 + [VMEM] * 5,
        out_specs=(VMEM,) * 9,
        cost_estimate=pl.CostEstimate(flops=100000, bytes_accessed=2000000, transcendentals=0),
    )(
        active_blocks, patience, productivity, income_levels, income_transition, wage_path, assignment, by_income,
        initial_mass, price_guess.reshape(1, PERIODS), jac_inverse, bond_supply.reshape(1, PERIODS),
    )
    price_row, jac, supply_row = near(price_row), near(jac), near(supply_row)
    shared = [near(array) for array in shared]
    sent, by_row = pl.pallas_call(
        first_kernel,
        name="first_round",
        out_shape=(pltpu.VMEM((1, PERIODS), f32), pltpu.VMEM((PERIODS, ROWS, BLOCK), i32)),
        in_specs=[VMEM] * 7,
        out_specs=(VMEM,) * 2,
        scratch_shapes=work,
    )(near(own), theirs, *shared, price_row)
    totals = exchanged(sent)
    sent, first_gap = pl.pallas_call(
        functools.partial(second_kernel, half_types=half_types, all_types=all_types),
        name="second_round",
        out_shape=(pltpu.VMEM((1, half_types * 2 * PERIODS), f32), pltpu.VMEM((1, PERIODS), f32)),
        in_specs=[VMEM] * 9,
        out_specs=(VMEM,) * 2,
        scratch_shapes=work,
    )(near(by_row), *shared, price_row, jac, supply_row, totals)
    everything = exchanged(sent)
    price_path, market_gap, type_paths = pl.pallas_call(
        functools.partial(last_kernel, half_types=half_types, all_types=all_types),
        name="last_update",
        out_shape=(
            jax.ShapeDtypeStruct((1, PERIODS), f32),
            jax.ShapeDtypeStruct((1, PERIODS), f32),
            jax.ShapeDtypeStruct((local_types, 2, PERIODS), f32),
        ),
        in_specs=[VMEM] * 6,
        out_specs=(VMEM,) * 3,
    )(near(wanted), price_row, jac, supply_row, near(first_gap), everything)
    return price_path.reshape(PERIODS), market_gap.reshape(PERIODS), type_paths


def solution(mesh):
    torus = Mesh(
        mesh.devices.reshape(4, 8, 4, mesh.shape["tm"]), ("types_0", "types_1", "types_2", "tm")
    )
    in_specs = (
        P(TYPES, "tm", None, None),
        P(TYPES),
        P(TYPES, None, None),
        P(TYPES),
        P(TYPES),
        P(),
        P(),
        P(),
        P(),
        P(),
        P(),
        P(),
    )
    out_specs = (P(), P(), P(TYPES, None, None))
    return jax.shard_map(body, mesh=torus, in_specs=in_specs, out_specs=out_specs, check_vma=False)
```

time: 61.1 us -> 57.6 us (0.943)
  Pallas kernels: 11.7 us -> 9.45 us
  waiting for transfers between devices: 1.49 us -> 0.22 us
    pallas_call x1, Pallas kernels: 5.11 us -> 3.6 us  [body(): pl.pallas_call(first_kernel, name='first_round', out_shape=(pltpu.VMEM((1...]
    ppermute x1, waiting for transfers between devices: 1.49 us -> 0.22 us  [body(): lax.ppermute(by_income, 'tm', [(c, cores - 1 - c) for c in range(cores)])]
    pallas_call x0 -> x1, Pallas kernels: none -> 1.26 us  [body(): pl.pallas_call(start_kernel, name='start', out_shape=(pltpu.VMEM((HALF, R...]
    pallas_call x1, Pallas kernels: 4.87 us -> 3.69 us  [body(): pl.pallas_call(functools.partial(second_kernel, half_types=half_types, al...]
    pallas_call x1, Pallas kernels: 1.69 us -> 0.9 us  [body(): pl.pallas_call(functools.partial(last_kernel, half_types=half_types, all_...]
  transfers between devices with their start and end apart: 1 -> 1, of which waited for: 1 -> 1; matrix products, arithmetic and copies ran while one was open for 0% -> 0% of each run, Pallas kernels for 0% -> 2%
where the time goes in v3:
time: 57.6 us; the launch traced here: 57.4 us
  blocking collectives  43.6 us (76%)
  Pallas kernels  9.45 us (16%)
  starting transfers between devices  3.33 us (6%)
  between operations  0.67 us (1%)
    all_to_all x2, blocking collectives, exchanged(): lax.all_to_all(copies, EVERY, split_axis=0, concat_axis=0, tiled=True)  43.6 us
    pallas_call x1, Pallas kernels, body(): pl.pallas_call(functools.partial(second_kernel, half_types=half_types, al...  3.69 us
    pallas_call x1, Pallas kernels, body(): pl.pallas_call(first_kernel, name='first_round', out_shape=(pltpu.VMEM((1...  3.6 us
    ppermute x1, starting transfers between devices, body(): lax.ppermute(by_income, 'tm', [(c, cores - 1 - c) for c in range(cores)])  3.33 us
    pallas_call x1, Pallas kernels, body(): pl.pallas_call(start_kernel, name='start', out_shape=(pltpu.VMEM((HALF, R...  1.26 us
  transfers between devices with their start and end apart: 1, of which 1 were waited for; matrix products, arithmetic and copies ran while one was open for 0% of the time, Pallas kernels for 2%

profile of v3, /device:TPU:1, one launch (start us, length us, event | category | flops | bytes accessed | tf_op | source)
XLA Modules:
  0.0 57.4 jit_solution(9280943360949011859)
XLA Ops:
  0.6 3.3 %collective-permute-start = (s32[2,3,7,4,512]{4,3,2,1,0:T(4,128)}, s32[2,3,7,4,512]{4,3,2,1,0:T(4,128)S(1)}, u32[]{:S(2)}, u32[]{:S(2)}) collective-permute-start(s32[2,3,7,4,512]{4,3,2,1,0:T(4,128)} %bitcast.15), channel_id=1, source_target_pairs={{0,1},{1,0},{2,3},{3,2},{4,5},{5,4},{6,7},{7,6},{8,9},{9,8},{10,11... | collective-permute-start | bytes 1032200 | tf_op jit(solution)/shard_map/ppermute | solution.py:329
  4.0 1.3 %start.1 = (s32[4,88,128]{2,1,0:T(8,128)S(1)}, f32[88,128]{1,0:T(8,128)S(1)}, f32[64,128]{1,0:T(8,128)S(1)}, f32[88,128]{1,0:T(8,128)S(1)}, f32[88,128]{1,0:T(8,...) custom-call(s32[6]{0:T(128)} %blocks.1, f32[6]{0:T(128)} %patience.1, ...), custom_call_target="tpu_custom_call" | custom-call | flops 100000 | bytes 2000000 | tf_op jit(solution)/shard_map/start/pallas_call | solution.py:345
  5.2 0.2 collective-permute-done.theirs
  5.5 3.6 %first_round.1 = (f32[1,8]{1,0:T(1,128)S(1)}, s32[8,88,128]{2,1,0:T(8,128)S(1)}) custom-call(s32[4,88,128]{2,1,0:T(8,128)S(1)} %get-tuple-element.23.own, s32[2,3,7,4,512]{4,3,2,1,0:T(4,128)S(1)} %collective-permute-done.theirs, f32[88,128]{1,0:T(8,128)S(1)} %get-tuple-element.24.start, f32[64,128]{1,0:T(8,128)S(1)} %get-tuple-element.25.consts, ...), custom_call_target="tpu_custom_call" | custom-call | tf_op jit(solution)/shard_map/first_round/pallas_call | solution.py:368
  9.1 0.1 broadcast_in_dim.17
  9.1 25.5 %all_to_all.10 = f32[256,1,8]{2,1,0:T(1,128)S(1)} all-to-all(f32[256,1,8]{2,1,0:T(1,128)S(1)} %broadcast_in_dim.17), channel_id=1, replica_groups=mesh['types_0'=4,'types_1'=8,'types_2'=4,'tm'=2] {'types_0','types_1','t..., dimensions={0} | all-to-all | bytes 16384 | tf_op jit(solution)/shard_map/all_to_all | solution.py:333
  34.6 3.7 %second_round.1 = (f32[1,48]{1,0:T(1,128)S(1)}, f32[1,8]{1,0:T(1,128)S(1)}) custom-call(s32[8,88,128]{2,1,0:T(8,128)S(1)} %get-tuple-element.28.brackets, f32[88,128]{1,0:T(8,128)S(1)} %get-tuple-element.24.start, f32[64,128]{1,0:T(8,128)S(1)} %get-tuple-element.25.consts, f32[88,128]{1,0:T(8,128)S(1)} %get-tuple-element.26.beta, ...), custom_call_target="tpu_custom_call" | custom-call | tf_op jit(solution)/shard_map/second_round/pallas_call | solution.py:377
  38.3 0.1 broadcast_in_dim.19
  38.4 18.2 %all_to_all.11 = f32[256,1,48]{2,1,0:T(1,128)S(1)} all-to-all(f32[256,1,48]{2,1,0:T(1,128)S(1)} %broadcast_in_dim.19), channel_id=1, replica_groups=mesh['types_0'=4,'types_1'=8,'types_2'=4,'tm'=2] {'types_0','types_1','t..., dimensions={0} | all-to-all | bytes 98304 | tf_op jit(solution)/shard_map/all_to_all | solution.py:333
  56.5 0.9 %last_update.1 = (f32[1,8]{1,0:T(1,128)}, f32[1,8]{1,0:T(1,128)}, f32[6,2,8]{2,1,0:T(2,128)}) custom-call(s32[8,128]{1,0:T(8,128)S(1)} %get-tuple-element.19.wanted, f32[1,8]{1,0:T(1,128)S(1)} %get-tuple-element.20.price, f32[8,8]{1,0:T(8,128)S(1)} %get-tuple-element.21.jac, f32[1,8]{1,0:T(1,128)S(1)} %get-tuple-element.22.supply, ...), custom_call_target="tpu_custom_call" | custom-call | tf_op jit(solution)/shard_map/last_update/pallas_call | solution.py:386
Async XLA Ops:
  0.6 4.8 %collective-permute-start = (s32[2,3,7,4,512]{4,3,2,1,0:T(4,128)}, s32[2,3,7,4,512]{4,3,2,1,0:T(4,128)S(1)}, u32[]{:S(2)}, u32[]{:S(2)}) collective-permute-start(s32[2,3,7,4,512]{4,3,2,1,0:T(4,128)} %bitcast.15), channel_id=1, source_target_pairs={{0,1},{1,0},{2,3},{3,2},{4,5},{5,4},{6,7},{7,6},{8,9},{9,8},{10,11... | collective-permute-start | bytes 1032200 | tf_op jit(solution)/shard_map/ppermute | solution.py:329

commit v4 on v3

--- a/solution.py
+++ b/solution.py
@@ -84,12 +84,13 @@
 def mix(source, target, consts, offset, transposed):
     states = [source(e) for e in range(INCOME)]
     for e in range(INCOME):
-        total = None
+        terms = []
         for f in range(INCOME):
             at = f * INCOME + e if transposed else e * INCOME + f
-            term = splat(consts[pl.ds(at, 1), :], WIDE) * states[f]
-            total = term if total is None else total + term
-        target[pl.ds(offset + e * SHARE, WIDE), :] = total
+            terms.append(splat(consts[pl.ds(at, 1), :], WIDE) * states[f])
+        while len(terms) > 1:
+            terms = [sum(terms[i + 1 : i + 2], terms[i]) for i in range(0, len(terms), 2)]
+        target[pl.ds(offset + e * SHARE, WIDE), :] = terms[0]
 
 
 def solve(consts, beta, pay, brackets, start, rates, weights, savings, values, edges, masses, crossings, series, full):
@@ -137,14 +138,14 @@
             low = grid_scale * place * place
             width = grid_scale * (2.0 * place + 1.0)
             spacing = jnp.maximum(upper - lower, width * inverse)
-            weight = jnp.clip((grid - lower) / spacing, 0.0, 1.0)
-            saved = low + weight * width
+            reached = jnp.clip(grid - lower, 0.0, spacing)
+            values[rows_of(c), :] = (1.0 + rate) * spacing / ((budget + income - low) * spacing - reached * width)
+            weight = reached / spacing
             weights[t, rows_of(c), :] = weight
-            savings[t, rows_of(c), :] = saved
-            values[rows_of(c), :] = (1.0 + rate) / (budget + income - saved)
+            savings[t, rows_of(c), :] = low + weight * width
         return carried
 
-    lax.fori_loop(0, PERIODS, backward, 0)
+    lax.fori_loop(0, PERIODS, backward, 0, unroll=4)
     for c in range(CHUNKS):
         masses[rows_of(c), :] = start[rows_of(c), :]
 
@@ -177,13 +178,15 @@
             hit = [drop == s for s in range(REACH + 2)]
             here = jnp.where(hit[0], staying, jnp.where(hit[1], rising, 0.0))
             here = here + pltpu.roll(jnp.where(hit[0], rising, 0.0), 1, 1)
-            crossed = jnp.zeros((TILE, BLOCK), jnp.float32)
+            parts = []
             for s in range(1, REACH + 2):
                 moved = jnp.where(hit[s], staying, jnp.where(hit[s + 1], rising, 0.0) if s <= REACH else 0.0)
                 moved = pltpu.roll(moved, BLOCK - s, 1)
                 inside = lane < BLOCK - s
-                here = here + jnp.where(inside, moved, 0.0)
-                crossed = crossed + jnp.where(inside, 0.0, moved)
+                parts.append((jnp.where(inside, moved, 0.0), jnp.where(inside, 0.0, moved)))
+            while len(parts) > 1:
+                parts = [tuple(sum(z[1:], z[0]) for z in zip(*parts[i : i + 2])) for i in range(0, len(parts), 2)]
+            here, crossed = here + parts[0][0], parts[0][1]
             edges[rows_of(c), :] = here
             crossings[rows_of(c), :] = crossed
 
@@ -193,7 +196,7 @@
         mix(arrived, masses, consts, 0, True)
         return carried
 
-    lax.fori_loop(0, PERIODS - 1, forward, 0)
+    lax.fori_loop(0, PERIODS - 1, forward, 0, unroll=True)
     sums(PERIODS - 1)
 
 

time: 57.6 us -> 57.2 us (level)
  no operation moved by 1% of the time
where the time goes in v4:
time: 57.2 us; the launch traced here: 57 us
  blocking collectives  43.6 us (76%)
  Pallas kernels  9.08 us (16%)
  starting transfers between devices  3.33 us (6%)
  between operations  0.66 us (1%)
    all_to_all x2, blocking collectives, exchanged(): lax.all_to_all(copies, EVERY, split_axis=0, concat_axis=0, tiled=True)  43.6 us
    pallas_call x1, Pallas kernels, body(): pl.pallas_call(functools.partial(second_kernel, half_types=half_types, al...  3.51 us
    pallas_call x1, Pallas kernels, body(): pl.pallas_call(first_kernel, name='first_round', out_shape=(pltpu.VMEM((1...  3.41 us
    ppermute x1, starting transfers between devices, body(): lax.ppermute(by_income, 'tm', [(c, cores - 1 - c) for c in range(cores)])  3.33 us
    pallas_call x1, Pallas kernels, body(): pl.pallas_call(start_kernel, name='start', out_shape=(pltpu.VMEM((HALF, R...  1.26 us
  transfers between devices with their start and end apart: 1, of which 1 were waited for; matrix products, arithmetic and copies ran while one was open for 0% of the time, Pallas kernels for 2%

profile of v4, /device:TPU:1, one launch (start us, length us, event | category | flops | bytes accessed | tf_op | source)
XLA Modules:
  0.0 57.0 jit_solution(13817932157799672587)
XLA Ops:
  0.6 3.3 %collective-permute-start = (s32[2,3,7,4,512]{4,3,2,1,0:T(4,128)}, s32[2,3,7,4,512]{4,3,2,1,0:T(4,128)S(1)}, u32[]{:S(2)}, u32[]{:S(2)}) collective-permute-start(s32[2,3,7,4,512]{4,3,2,1,0:T(4,128)} %bitcast.15), channel_id=1, source_target_pairs={{0,1},{1,0},{2,3},{3,2},{4,5},{5,4},{6,7},{7,6},{8,9},{9,8},{10,11... | collective-permute-start | bytes 1032200 | tf_op jit(solution)/shard_map/ppermute | solution.py:332
  4.0 1.3 %start.1 = (s32[4,88,128]{2,1,0:T(8,128)S(1)}, f32[88,128]{1,0:T(8,128)S(1)}, f32[64,128]{1,0:T(8,128)S(1)}, f32[88,128]{1,0:T(8,128)S(1)}, f32[88,128]{1,0:T(8,...) custom-call(s32[6]{0:T(128)} %blocks.1, f32[6]{0:T(128)} %patience.1, ...), custom_call_target="tpu_custom_call" | custom-call | flops 100000 | bytes 2000000 | tf_op jit(solution)/shard_map/start/pallas_call | solution.py:348
  5.2 0.2 collective-permute-done.theirs
  5.5 3.4 %first_round.1 = (f32[1,8]{1,0:T(1,128)S(1)}, s32[8,88,128]{2,1,0:T(8,128)S(1)}) custom-call(s32[4,88,128]{2,1,0:T(8,128)S(1)} %get-tuple-element.23.own, s32[2,3,7,4,512]{4,3,2,1,0:T(4,128)S(1)} %collective-permute-done.theirs, f32[88,128]{1,0:T(8,128)S(1)} %get-tuple-element.24.start, f32[64,128]{1,0:T(8,128)S(1)} %get-tuple-element.25.consts, ...), custom_call_target="tpu_custom_call" | custom-call | tf_op jit(solution)/shard_map/first_round/pallas_call | solution.py:371
  8.9 0.1 broadcast_in_dim.17
  8.9 25.5 %all_to_all.10 = f32[256,1,8]{2,1,0:T(1,128)S(1)} all-to-all(f32[256,1,8]{2,1,0:T(1,128)S(1)} %broadcast_in_dim.17), channel_id=1, replica_groups=mesh['types_0'=4,'types_1'=8,'types_2'=4,'tm'=2] {'types_0','types_1','t..., dimensions={0} | all-to-all | bytes 16384 | tf_op jit(solution)/shard_map/all_to_all | solution.py:336
  34.4 3.5 %second_round.1 = (f32[1,48]{1,0:T(1,128)S(1)}, f32[1,8]{1,0:T(1,128)S(1)}) custom-call(s32[8,88,128]{2,1,0:T(8,128)S(1)} %get-tuple-element.28.brackets, f32[88,128]{1,0:T(8,128)S(1)} %get-tuple-element.24.start, f32[64,128]{1,0:T(8,128)S(1)} %get-tuple-element.25.consts, f32[88,128]{1,0:T(8,128)S(1)} %get-tuple-element.26.beta, ...), custom_call_target="tpu_custom_call" | custom-call | tf_op jit(solution)/shard_map/second_round/pallas_call | solution.py:380
  37.9 0.1 broadcast_in_dim.19
  38.0 18.2 %all_to_all.11 = f32[256,1,48]{2,1,0:T(1,128)S(1)} all-to-all(f32[256,1,48]{2,1,0:T(1,128)S(1)} %broadcast_in_dim.19), channel_id=1, replica_groups=mesh['types_0'=4,'types_1'=8,'types_2'=4,'tm'=2] {'types_0','types_1','t..., dimensions={0} | all-to-all | bytes 98304 | tf_op jit(solution)/shard_map/all_to_all | solution.py:336
  56.1 0.9 %last_update.1 = (f32[1,8]{1,0:T(1,128)}, f32[1,8]{1,0:T(1,128)}, f32[6,2,8]{2,1,0:T(2,128)}) custom-call(s32[8,128]{1,0:T(8,128)S(1)} %get-tuple-element.19.wanted, f32[1,8]{1,0:T(1,128)S(1)} %get-tuple-element.20.price, f32[8,8]{1,0:T(8,128)S(1)} %get-tuple-element.21.jac, f32[1,8]{1,0:T(1,128)S(1)} %get-tuple-element.22.supply, ...), custom_call_target="tpu_custom_call" | custom-call | tf_op jit(solution)/shard_map/last_update/pallas_call | solution.py:389
Async XLA Ops:
  0.6 4.8 %collective-permute-start = (s32[2,3,7,4,512]{4,3,2,1,0:T(4,128)}, s32[2,3,7,4,512]{4,3,2,1,0:T(4,128)S(1)}, u32[]{:S(2)}, u32[]{:S(2)}) collective-permute-start(s32[2,3,7,4,512]{4,3,2,1,0:T(4,128)} %bitcast.15), channel_id=1, source_target_pairs={{0,1},{1,0},{2,3},{3,2},{4,5},{5,4},{6,7},{7,6},{8,9},{9,8},{10,11... | collective-permute-start | bytes 1032200 | tf_op jit(solution)/shard_map/ppermute | solution.py:332

commit v5 on v4

--- a/solution.py
+++ b/solution.py
@@ -202,9 +202,10 @@
 
 def start_kernel(
     blocks, patience, productivity, levels, transition, wage, assignment, mine, mass, price_in, jac_in, supply_in,
-    own, start, consts, beta, pay, wanted, price, jac, supply,
+    own, start, consts, beta, pay, wanted, price, jac, supply, rates,
 ):
     price[...], jac[...], supply[...] = price_in[...], jac_in[...], supply_in[...]
+    set_rates(price_column(price_in[...], None, ()), rates)
     half_types = mine.shape[1]
     core = lax.axis_index("tm")
     here = lax.axis_index(TYPES)
@@ -238,8 +239,8 @@
 
 
 def first_kernel(
-    own, theirs, start, consts, beta, pay, price,
-    out, brackets, rates, weights, savings, values, edges, masses, crossings, series,
+    own, theirs, start, consts, beta, pay, rates,
+    out, brackets, weights, savings, values, edges, masses, crossings, series,
 ):
     half_types = theirs.shape[1]
     core = lax.axis_index("tm")
@@ -252,7 +253,6 @@
                 line, part = pl.ds(e * SHARE + k * BLOCKS + b, 1), pl.ds(b * BLOCK, BLOCK)
                 for t in range(HALF):
                     brackets[(1 - core) * HALF + t, line, :] = theirs[core, k, e, pl.ds(t, 1), part]
-    set_rates(price_column(price[...], None, ()), rates)
     solve(consts, beta, pay, brackets, start, rates, weights, savings, values, edges, masses, crossings, series, False)
     lane = iota(1)
     held = jnp.zeros((TILE, BLOCK), jnp.float32)
@@ -345,7 +345,7 @@
         pltpu.VMEM((DEEP, BLOCK), f32),
         pltpu.VMEM((2, PERIODS, FRAME, BLOCK), f32),
     ]
-    own, *shared, wanted, price_row, jac, supply_row = pl.pallas_call(
+    own, *shared, wanted, price_row, jac, supply_row, first_rates = pl.pallas_call(
         start_kernel,
         name="start",
         out_shape=(
@@ -358,9 +358,10 @@
             pltpu.VMEM((1, PERIODS), f32),
             pltpu.VMEM((PERIODS, PERIODS), f32),
             pltpu.VMEM((1, PERIODS), f32),
+            pltpu.VMEM((2, PERIODS, BLOCK), f32),
         ),
         in_specs=[SMEM] * 7 + [VMEM] * 5,
-        out_specs=(VMEM,) * 9,
+        out_specs=(VMEM,) * 10,
         cost_estimate=pl.CostEstimate(flops=100000, bytes_accessed=2000000, transcendentals=0),
     )(
         active_blocks, patience, productivity, income_levels, income_transition, wage_path, assignment, by_income,
@@ -374,8 +375,8 @@
         out_shape=(pltpu.VMEM((1, PERIODS), f32), pltpu.VMEM((PERIODS, ROWS, BLOCK), i32)),
         in_specs=[VMEM] * 7,
         out_specs=(VMEM,) * 2,
-        scratch_shapes=work,
-    )(near(own), theirs, *shared, price_row)
+        scratch_shapes=work[1:],
+    )(near(own), theirs, *shared, near(first_rates))
     totals = exchanged(sent)
     sent, first_gap = pl.pallas_call(
         functools.partial(second_kernel, half_types=half_types, all_types=all_types),

time: 57.2 us -> 57.2 us (level)
  no operation moved by 1% of the time
where the time goes in v5:
time: 57.2 us; the launch traced here: 57 us
  blocking collectives  43.6 us (76%)
  Pallas kernels  9.04 us (16%)
  starting transfers between devices  3.33 us (6%)
  between operations  0.66 us (1%)
    all_to_all x2, blocking collectives, exchanged(): lax.all_to_all(copies, EVERY, split_axis=0, concat_axis=0, tiled=True)  43.6 us
    pallas_call x1, Pallas kernels, body(): pl.pallas_call(functools.partial(second_kernel, half_types=half_types, al...  3.51 us
    pallas_call x1, Pallas kernels, body(): pl.pallas_call(first_kernel, name='first_round', out_shape=(pltpu.VMEM((1...  3.37 us
    ppermute x1, starting transfers between devices, body(): lax.ppermute(by_income, 'tm', [(c, cores - 1 - c) for c in range(cores)])  3.33 us
    pallas_call x1, Pallas kernels, body(): pl.pallas_call(start_kernel, name='start', out_shape=(pltpu.VMEM((HALF, R...  1.26 us
  transfers between devices with their start and end apart: 1, of which 1 were waited for; matrix products, arithmetic and copies ran while one was open for 0% of the time, Pallas kernels for 2%

profile of v5, /device:TPU:1, one launch (start us, length us, event | category | flops | bytes accessed | tf_op | source)
XLA Modules:
  0.0 57.0 jit_solution(1897873675108194221)
XLA Ops:
  0.6 3.3 %collective-permute-start = (s32[2,3,7,4,512]{4,3,2,1,0:T(4,128)}, s32[2,3,7,4,512]{4,3,2,1,0:T(4,128)S(1)}, u32[]{:S(2)}, u32[]{:S(2)}) collective-permute-start(s32[2,3,7,4,512]{4,3,2,1,0:T(4,128)} %bitcast.15), channel_id=1, source_target_pairs={{0,1},{1,0},{2,3},{3,2},{4,5},{5,4},{6,7},{7,6},{8,9},{9,8},{10,11... | collective-permute-start | bytes 1032200 | tf_op jit(solution)/shard_map/ppermute | solution.py:332
  4.0 1.3 %start.1 = (s32[4,88,128]{2,1,0:T(8,128)S(1)}, f32[88,128]{1,0:T(8,128)S(1)}, f32[64,128]{1,0:T(8,128)S(1)}, f32[88,128]{1,0:T(8,128)S(1)}, f32[88,128]{1,0:T(8,...) custom-call(s32[6]{0:T(128)} %blocks.1, ...), custom_call_target="tpu_custom_call" | custom-call | flops 100000 | bytes 2000000 | tf_op jit(solution)/shard_map/start/pallas_call | solution.py:348
  5.2 0.2 collective-permute-done.theirs
  5.5 3.4 %first_round.1 = (f32[1,8]{1,0:T(1,128)S(1)}, s32[8,88,128]{2,1,0:T(8,128)S(1)}) custom-call(s32[4,88,128]{2,1,0:T(8,128)S(1)} %get-tuple-element.24.own, s32[2,3,7,4,512]{4,3,2,1,0:T(4,128)S(1)} %collective-permute-done.theirs, f32[88,128]{1,0:T(8,128)S(1)} %get-tuple-element.25.start, f32[64,128]{1,0:T(8,128)S(1)} %get-tuple-element.26.consts, ...), custom_call_target="tpu_custom_call" | custom-call | tf_op jit(solution)/shard_map/first_round/pallas_call | solution.py:372
  8.8 0.1 broadcast_in_dim.17
  8.9 25.5 %all_to_all.10 = f32[256,1,8]{2,1,0:T(1,128)S(1)} all-to-all(f32[256,1,8]{2,1,0:T(1,128)S(1)} %broadcast_in_dim.17), channel_id=1, replica_groups=mesh['types_0'=4,'types_1'=8,'types_2'=4,'tm'=2] {'types_0','types_1','t..., dimensions={0} | all-to-all | bytes 16384 | tf_op jit(solution)/shard_map/all_to_all | solution.py:336
  34.4 3.5 %second_round.1 = (f32[1,48]{1,0:T(1,128)S(1)}, f32[1,8]{1,0:T(1,128)S(1)}) custom-call(s32[8,88,128]{2,1,0:T(8,128)S(1)} %get-tuple-element.30.brackets, f32[88,128]{1,0:T(8,128)S(1)} %get-tuple-element.25.start, f32[64,128]{1,0:T(8,128)S(1)} %get-tuple-element.26.consts, f32[88,128]{1,0:T(8,128)S(1)} %get-tuple-element.27.beta, ...), custom_call_target="tpu_custom_call" | custom-call | tf_op jit(solution)/shard_map/second_round/pallas_call | solution.py:381
  37.9 0.1 broadcast_in_dim.19
  38.0 18.2 %all_to_all.11 = f32[256,1,48]{2,1,0:T(1,128)S(1)} all-to-all(f32[256,1,48]{2,1,0:T(1,128)S(1)} %broadcast_in_dim.19), channel_id=1, replica_groups=mesh['types_0'=4,'types_1'=8,'types_2'=4,'tm'=2] {'types_0','types_1','t..., dimensions={0} | all-to-all | bytes 98304 | tf_op jit(solution)/shard_map/all_to_all | solution.py:336
  56.1 0.9 %last_update.1 = (f32[1,8]{1,0:T(1,128)}, f32[1,8]{1,0:T(1,128)}, f32[6,2,8]{2,1,0:T(2,128)}) custom-call(s32[8,128]{1,0:T(8,128)S(1)} %get-tuple-element.20.wanted, f32[1,8]{1,0:T(1,128)S(1)} %get-tuple-element.21.price, f32[8,8]{1,0:T(8,128)S(1)} %get-tuple-element.22.jac, f32[1,8]{1,0:T(1,128)S(1)} %get-tuple-element.23.supply, ...), custom_call_target="tpu_custom_call" | custom-call | tf_op jit(solution)/shard_map/last_update/pallas_call | solution.py:390
Async XLA Ops:
  0.6 4.8 %collective-permute-start = (s32[2,3,7,4,512]{4,3,2,1,0:T(4,128)}, s32[2,3,7,4,512]{4,3,2,1,0:T(4,128)S(1)}, u32[]{:S(2)}, u32[]{:S(2)}) collective-permute-start(s32[2,3,7,4,512]{4,3,2,1,0:T(4,128)} %bitcast.15), channel_id=1, source_target_pairs={{0,1},{1,0},{2,3},{3,2},{4,5},{5,4},{6,7},{7,6},{8,9},{9,8},{10,11... | collective-permute-start | bytes 1032200 | tf_op jit(solution)/shard_map/ppermute | solution.py:332
